TPU v7x, 128 devices: a whole 4x4x4 slice. The times are simulated.
128 devices in a mesh: row: 8 (over y, z_lo), col: 16 (over z_hi, x, core).
Axes of the slice: x: 4, y: 4, z: 4 (z_hi: 2, z_lo: 2; z = z_hi * 2 + z_lo), core: 2. Of those that a mesh axis runs over, the one named last changes fastest.
Arguments:
- hidden: bfloat16 [5120, 5120], P('col'), may hold values from -26 to 26
- lengths: int32 [4], replicated, may hold values from 512 to 2048, as said below
- owner: int32 [4], replicated, may hold values from 0 to 15, as said below
- page_table: int32 [4, 16], replicated, may hold values from 0 to 15, as said below
- qkv_train: float32 [3, 5120, 3072], P(None, 'row', 'col'), may hold values from -1 to 1
- qk_gain: float32 [2, 3072], P(None, 'row'), may hold values from 0.1 to 1.9
- o_weight: bfloat16 [3072, 5120], P('row'), may hold values from -1.5 to 1.5
- post_gain: float32 [5120], P('row'), may hold values from 0.1 to 1.9
- gate_up_train: float32 [2, 5120, 13824], P(None, 'row', 'col'), may hold values from -0.078125 to 0.078125
Outputs:
- layer_out: bfloat16 [5120, 5120], P('col', 'row')
- kv_cache: bfloat16 [16, 16, 2, 128, 3072], P('col', None, None, None, 'row')
- qkv_server: bfloat16 [3, 8, 640, 3072], P(None, None, 'col', 'row')
- gate_up_server: bfloat16 [2, 8, 640, 13824], P(None, None, 'col', 'row')
Inputs may be any that keep to these rules, and one draw needn't show every extreme that they name: The lengths add up to 5120; one prompt has 2048 tokens and one 512. `owner`: the owners are distinct. `page_table`: each row is a permutation of the 16 slots.
All inputs are finite; a program needn't handle non-finite values.
Results may differ from a plain program's by a relative error of at most 0.025.
Values may be sent and summed in bfloat16 or wider, within the bound.
A program may use at most 128 MiB of HBM per device.

v0:
```python
import functools
import math

import jax
import jax.numpy as jnp
from jax import lax
from jax.experimental import pallas as pl
from jax.experimental.pallas import tpu as pltpu
from jax.sharding import PartitionSpec as P

HD = 128
HEADS = 24
PAGE = 128
PAGES = 16
LMAX = 2048

norm_epsilon = 1e-06
rope_theta = 500000.0
big_negative = -1e30


def inverse_rms(squares, features):
    return lax.rsqrt(squares / features + norm_epsilon)


def rotate_heads(inputs, positions):
    half_dim = inputs.shape[-1] // 2
    frequency = rope_theta ** (-2.0 * jnp.arange(half_dim, dtype=jnp.float32) / inputs.shape[-1])
    angles = positions.astype(jnp.float32)[:, None] * frequency[None, :]
    cosine = jnp.cos(angles)[:, None, :]
    sine_part = jnp.sin(angles)[:, None, :]
    lower_half = inputs[..., :half_dim]
    upper_half = inputs[..., half_dim:]
    return jnp.concatenate(
        [
            lower_half * cosine - upper_half * sine_part,
            upper_half * cosine + lower_half * sine_part,
        ],
        axis=-1,
    )


def locate_tokens(token_index, lengths):
    prompt_ends = jnp.cumsum(lengths)
    prompt_starts = prompt_ends - lengths
    segment = jnp.sum((token_index[:, None] >= prompt_ends[None, :]).astype(jnp.int32), axis=1)
    onehot = segment[:, None] == jnp.arange(lengths.shape[0], dtype=jnp.int32)[None, :]
    start = jnp.sum(jnp.where(onehot, prompt_starts[None, :], 0), axis=1)
    return start


ALIGN = 16
WINDOW = PAGE + ALIGN


def cache_body(meta_ref, kv_ref, out_ref):
    tokens = kv_ref.shape[1]
    start, length = meta_ref[0], meta_ref[1]

    @pl.loop(0, PAGES)
    def _(page):
        first = jnp.minimum(start + page * PAGE, tokens - 1)
        base = jnp.minimum((first // ALIGN) * ALIGN, tokens - WINDOW)
        base = pl.multiple_of(base, ALIGN)
        shift = first - base
        slot = meta_ref[2 + page]
        rows = lax.broadcasted_iota(jnp.int32, (PAGE, 1), 0) + page * PAGE
        inside = rows < length
        for part in range(2):
            piece = kv_ref[part, pl.ds(base, WINDOW), :].astype(jnp.float32)
            piece = pltpu.roll(piece, lax.rem(WINDOW - shift, WINDOW), 0)[:PAGE]
            out_ref[slot, part] = jnp.where(inside, piece, 0.0).astype(jnp.bfloat16)


def build_cache(meta, kv):
    width = kv.shape[2]
    return pl.pallas_call(
        cache_body,
        out_shape=jax.ShapeDtypeStruct((PAGES, 2, PAGE, width), jnp.bfloat16),
        in_specs=[
            pl.BlockSpec(memory_space=pltpu.SMEM),
            pl.BlockSpec(memory_space=pltpu.VMEM),
        ],
        out_specs=pl.BlockSpec(memory_space=pltpu.VMEM),
        compiler_params=pltpu.CompilerParams(vmem_limit_bytes=40 << 20),
        cost_estimate=pl.CostEstimate(flops=10_000_000, bytes_accessed=11_000_000, transcendentals=0),
        name="cache_pages",
    )(meta, kv)


def attend_body(first_ref, start_ref, query_ref, kv_ref, out_ref, *, span):
    rows = query_ref.shape[0]
    heads = query_ref.shape[1] // HD
    first_query, first_key = first_ref[0], first_ref[1]
    first_key = pl.multiple_of(first_key, 64)
    query_index = first_query + lax.broadcasted_iota(jnp.int32, (rows, 1), 0)
    key_index = first_key + lax.broadcasted_iota(jnp.int32, (1, span), 1)
    allowed = (key_index <= query_index) & (key_index >= start_ref[...])
    for head in range(heads):
        lanes = slice(head * HD, (head + 1) * HD)
        keys = kv_ref[0, pl.ds(first_key, span), lanes]
        values = kv_ref[1, pl.ds(first_key, span), lanes]
        scores = lax.dot_general(
            query_ref[:, lanes], keys, (((1,), (1,)), ((), ())), preferred_element_type=jnp.float32
        ) * (1.0 / math.sqrt(HD))
        scores = jnp.where(allowed, scores, big_negative)
        exponent = jnp.exp(scores - jnp.max(scores, axis=1, keepdims=True))
        total = jnp.sum(exponent, axis=1, keepdims=True)
        mixed = jnp.dot(exponent.astype(jnp.bfloat16), values, preferred_element_type=jnp.float32)
        out_ref[:, lanes] = (mixed / total).astype(jnp.bfloat16)


def attend(first, start, query, kv, span):
    return pl.pallas_call(
        functools.partial(attend_body, span=span),
        out_shape=jax.ShapeDtypeStruct(query.shape, jnp.bfloat16),
        in_specs=[pl.BlockSpec(memory_space=pltpu.SMEM)]
        + [pl.BlockSpec(memory_space=pltpu.VMEM)] * 3,
        out_specs=pl.BlockSpec(memory_space=pltpu.VMEM),
        compiler_params=pltpu.CompilerParams(vmem_limit_bytes=48 << 20),
        cost_estimate=pl.CostEstimate(
            flops=4 * query.shape[0] * span * query.shape[1],
            bytes_accessed=8_000_000,
            transcendentals=3 * query.shape[0] * span,
        ),
        name="attend",
    )(first, start, query, kv)


def local(
    hidden, lengths, owner, page_table, qkv_train, qk_gain, o_weight, post_gain, gate_up_train
):
    n_row = lax.axis_size("row")
    n_col = lax.axis_size("col")
    col_index = lax.axis_index("col")
    row_index = lax.axis_index("row")
    tok_rows = hidden.shape[0]
    model_width = hidden.shape[1]
    row_width = model_width // n_row
    col_block = row_width // n_col
    trainer_qkv = qkv_train.astype(jnp.bfloat16)
    trainer_gate_up = gate_up_train.astype(jnp.bfloat16)
    server_qkv, server_gate_up = (
        lax.all_to_all(
            lax.all_to_all(trainer_qkv, "col", split_axis=1, concat_axis=2, tiled=True),
            "row",
            split_axis=2,
            concat_axis=1,
            tiled=True,
        ),
        lax.all_to_all(
            lax.all_to_all(trainer_gate_up, "col", split_axis=1, concat_axis=2, tiled=True),
            "row",
            split_axis=2,
            concat_axis=1,
            tiled=True,
        ),
    )
    heads_width = server_qkv.shape[2]
    local_heads = heads_width // HD
    weight_blocks = server_qkv.reshape(3, n_row, col_block, heads_width)
    gate_up_blocks = server_gate_up.reshape(2, n_row, col_block, server_gate_up.shape[2])
    hidden_three = hidden.reshape(tok_rows, n_row, row_width)
    shard_piece = lax.all_gather(weight_blocks, "col", axis=2, tiled=True)
    shards = shard_piece.shape[2] // col_block
    projected = jnp.einsum(
        "trb,jrbh->tjh", hidden_three, shard_piece, preferred_element_type=jnp.float32
    )
    query_rows = projected[:, 0]
    key_rows = projected[:, 1]
    value_rows = projected[:, 2]
    query_squares, key_squares = lax.psum(
        (jnp.sum(query_rows * query_rows, axis=1), jnp.sum(key_rows * key_rows, axis=1)), "row"
    )
    full_heads = HEADS * HD
    query_norm = query_rows * inverse_rms(query_squares, full_heads)[:, None] * qk_gain[0]
    key_norm = key_rows * inverse_rms(key_squares, full_heads)[:, None] * qk_gain[1]
    token_index = col_index * tok_rows + jnp.arange(tok_rows, dtype=jnp.int32)
    token_start = locate_tokens(token_index, lengths)
    position = token_index - token_start
    query_rot = rotate_heads(query_norm.reshape(tok_rows, local_heads, HD), position).astype(
        jnp.bfloat16
    ).reshape(tok_rows, heads_width)
    key_rot = (
        rotate_heads(key_norm.reshape(tok_rows, local_heads, HD), position)
        .astype(jnp.bfloat16)
        .reshape(tok_rows, heads_width)
    )
    value_flat = value_rows.astype(jnp.bfloat16)
    kv = lax.all_gather(jnp.stack([key_rot, value_flat]), "col", axis=1, tiled=True)

    prompt_starts = jnp.cumsum(lengths) - lengths
    owned = owner == col_index
    my_start = jnp.sum(jnp.where(owned, prompt_starts, 0))
    my_length = jnp.sum(jnp.where(owned, lengths, 0))
    my_pages = jnp.where(
        jnp.any(owned),
        jnp.sum(jnp.where(owned[:, None], page_table, 0), axis=0),
        jnp.arange(PAGES, dtype=jnp.int32),
    )
    meta = jnp.concatenate([jnp.stack([my_start, my_length]), my_pages]).astype(jnp.int32)
    cache_pages = build_cache(meta, kv)

    reach = -(-(LMAX - 1) // tok_rows)
    span = min(reach + 1, n_col) * tok_rows
    first_key = jnp.maximum(col_index - reach, 0) * tok_rows
    first = jnp.stack([col_index * tok_rows, first_key]).astype(jnp.int32)
    attention = attend(first, token_start[:, None], query_rot, kv, span)

    o_columns = lax.all_to_all(o_weight, "row", split_axis=1, concat_axis=0, tiled=True)
    attention_all = lax.all_gather(attention, "row", axis=1, tiled=True)
    own_out = jnp.dot(attention_all, o_columns, preferred_element_type=jnp.float32)
    out_squares = lax.psum(jnp.sum(own_out * own_out, axis=1), "row")
    normalized = own_out * inverse_rms(out_squares, model_width)[:, None] * post_gain
    residual = lax.dynamic_slice_in_dim(hidden, row_index * row_width, row_width, 1).astype(
        jnp.float32
    )
    layer_out = (residual + normalized).astype(jnp.bfloat16)
    return (layer_out, cache_pages[None], weight_blocks, gate_up_blocks)


def solution(mesh):
    in_specs = (
        P("col", None),
        P(),
        P(),
        P(),
        P(None, "row", "col"),
        P(None, "row"),
        P("row", None),
        P("row"),
        P(None, "row", "col"),
    )
    out_specs = (
        P("col", "row"),
        P("col", None, None, None, "row"),
        P(None, None, "col", "row"),
        P(None, None, "col", "row"),
    )
    return jax.shard_map(local, mesh=mesh, in_specs=in_specs, out_specs=out_specs, check_vma=False)
```

profile of v0, /device:TPU:0, one launch (start us, length us, event | category | flops | bytes accessed | tf_op | source)
XLA Modules:
  0.0 464.8 jit_solution(14021942218270815738)
XLA Ops:
  7.2 1.5 convert_element_type.52
  9.9 28.2 %all_to_all.85 = bf16[3,640,192]{2,0,1:T(4,128)(2,1)S(1)} all-to-all(bf16[3,640,192]{2,0,1:T(4,128)(2,1)S(1)} %copy.80), channel_id=1, replica_groups=mesh['row'=8,'col'=16] {'col'}, dimensions={1} | all-to-all | bytes 1474560 | tf_op jit(solution)/shard_map/all_to_all | solution.py:145
  39.2 4.8 %copy.101 = bf16[3,40,16,192]{1,0,3,2:T(4,128)(2,1)S(1)} copy(bf16[3,40,16,192]{3,1,2,0:T(8,128)(2,1)} %bitcast.61) | data formatting | bytes 1474560 | tf_op jit(solution)/shard_map/all_to_all | solution.py:145
  44.0 4.9 %reshape.168 = bf16[8,2,23040]{2,1,0:T(2,128)(2,1)} reshape(bf16[3072,3,40]{2,1,0:T(4,128)(2,1)S(1)} %bitcast.57) | data formatting | bytes 1474560
  49.0 17.0 %all_to_all.86 = bf16[8,2,23040]{2,1,0:T(2,128)(2,1)} all-to-all(bf16[8,2,23040]{2,1,0:T(2,128)(2,1)} %reshape.168), channel_id=1, replica_groups=mesh['row'=8,'col'=16] {'row'}, dimensions={0} | all-to-all | bytes 1474560 | tf_op jit(solution)/shard_map/all_to_all | solution.py:144
  65.9 6.1 %reshape.169 = bf16[3072,3,40]{2,1,0:T(4,128)(2,1)S(1)} reshape(bf16[8,2,23040]{2,1,0:T(2,128)(2,1)} %all_to_all.86) | data formatting | bytes 1474560
  72.1 3.0 copy.85
  76.7 81.9 %all-gather.4.cloned.1.call-done = bf16[3,8,640,384]{3,2,1,0:T(8,128)(2,1)} async-done(((bf16[3,8,40,384]{3,2,1,0:T(8,128)(2,1)}), bf16[3,8,640,384]{3,2,1,0:T(8,128)(2,1)}) %all-gather.4.cloned.1.call-update) | async-done | bytes 11796496 | tf_op jit(solution)/shard_map/all_gather | solution.py:164
  158.6 9.0 %fusion.2 = f32[320,3,384]{2,0,1:T(8,128)S(1)} fusion(bf16[3,8,640,384]{3,2,1,0:T(8,128)(2,1)} %all-gather.4.cloned.1.call-done, bf16[40,8,8,640]{3,2,1,0:T(8,128)(2,1)} %bitcast.70), kind=kOutput, calls=%fused_computation.3 | convolution fusion | flops 3774873600 | bytes 16547840 | tf_op jit(solution)/shard_map/trb,jrbh->tjh/dot_general | solution.py:166
  168.3 18.8 %all-reduce = (f32[320]{0:T(512)S(1)}, f32[320]{0:T(512)S(1)}) all-reduce(f32[320]{0:T(512)S(1)} %get-tuple-element.25, f32[320]{0:T(512)S(1)} %get-tuple-element.24), channel_id=1, replica_groups=mesh['row'=8,'col'=16] {'row'}, use_global_device_ids=true, to_apply=%region_4.0 | all-reduce | flops 640 | bytes 5120 | tf_op jit(solution)/shard_map/psum | solution.py:172
  188.6 2.5 convert_element_type.58
  191.1 5.1 %copy.94 = bf16[2,640,864]{2,0,1:T(2,128)(2,1)} copy(bf16[2,640,864]{1,2,0:T(8,128)(2,1)S(1)} %convert_element_type.58) | data formatting | bytes 4423680 | tf_op jit(solution)/shard_map/convert_element_type | solution.py:142
  196.2 4.1 all-to-all-start.3
  200.4 6.3 %copy.92 = bf16[384,5120]{0,1:T(8,128)(2,1)} copy(bf16[384,5120]{1,0:T(8,128)(2,1)} %param.15) | data formatting | bytes 7864320 | tf_op args[6]
  206.7 28.2 %all-to-all-done.3 = bf16[2,640,864]{2,0,1:T(2,128)(2,1)S(1)} async-done(((bf16[2,640,864]{2,0,1:T(2,128)(2,1)}), bf16[2,640,864]{2,0,1:T(2,128)(2,1)S(1)}, u32[]{:S(2)}, u32[]{:S(2)}) %all-to-all-start.3) | async-done | bytes 2211872 | tf_op jit(solution)/shard_map/all_to_all | solution.py:152
  234.9 1.4 copy-done.1
  236.3 4.5 all-to-all-start.2
  241.5 76.1 %all-gather.6.cloned.1.call-done.kv_ref = bf16[2,5120,384]{2,1,0:T(8,128)(2,1)} async-done(((bf16[2,320,384]{2,1,0:T(8,128)(2,1)}), bf16[2,5120,384]{2,1,0:T(8,128)(2,1)}) %all-gather.6.cloned.1.call-update) | async-done | bytes 7864336 | tf_op jit(solution)/shard_map/all_gather | solution.py:190
  317.6 9.5 %attend.1 = bf16[320,384]{1,0:T(8,128)(2,1)} custom-call(s32[2]{0:T(128)S(1)} %pad_add_fusion.first_ref, s32[320,1]{1,0:T(8,128)S(1)} %broadcast_in_dim.60.start_ref, bf16[320,384]{1,0:T(8,128)(2,1)S(1)} %copy.91.query_ref, bf16[2,5120,384]{2,1,0:T(8,128)(2,1)} %all-gather.6.cloned.1.call-done.kv_ref), custom_call_target="tpu_custom_call" | custom-call | flops 1258291200 | bytes 8000000 | tf_op jit(solution)/shard_map/attend/pallas_call | solution.py:114
  327.1 1.9 copy.95
  329.1 12.8 %copy.104 = bf16[2,40,16,864]{1,0,3,2:T(2,128)(2,1)} copy(bf16[2,40,16,864]{3,1,2,0:T(8,128)(2,1)S(1)} %bitcast.59) | data formatting | bytes 4423680 | tf_op jit(solution)/shard_map/all_to_all | solution.py:152
  341.9 12.1 %reshape.170 = bf16[8,2,69120]{2,1,0:T(2,128)(2,1)} reshape(bf16[13824,2,40]{2,1,0:T(2,128)(2,1)} %bitcast.54) | data formatting | bytes 4423680
  354.0 4.7 %all-to-all-start.4 = ((bf16[8,2,69120]{2,1,0:T(2,128)(2,1)}), bf16[8,2,69120]{2,1,0:T(2,128)(2,1)S(1)}, u32[]{:S(2)}, u32[]{:S(2)}) async-start(bf16[8,2,69120]{2,1,0:T(2,128)(2,1)} %reshape.170), calls=%async_computation.4 | async-start | bytes 4423680 | tf_op jit(solution)/shard_map/all_to_all | solution.py:151
  361.4 6.3 %copy.93 = bf16[8,384,640]{2,1,0:T(8,128)(2,1)} copy(bf16[8,384,640]{1,2,0:T(8,128)(2,1)} %bitcast.18) | data formatting | bytes 7864320 | tf_op jit(solution)/shard_map/all_to_all | solution.py:210
  367.8 29.3 %all-to-all-done.4 = bf16[8,2,69120]{2,1,0:T(2,128)(2,1)S(1)} async-done(((bf16[8,2,69120]{2,1,0:T(2,128)(2,1)}), bf16[8,2,69120]{2,1,0:T(2,128)(2,1)S(1)}, u32[]{:S(2)}, u32[]{:S(2)}) %all-to-all-start.4) | async-done | bytes 2211872 | tf_op jit(solution)/shard_map/all_to_all | solution.py:151
  397.0 12.0 %reshape.171 = bf16[13824,2,40]{2,1,0:T(2,128)(2,1)} reshape(bf16[8,2,69120]{2,1,0:T(2,128)(2,1)S(1)} %all-to-all-done.4) | data formatting | bytes 4423680
  409.1 15.7 %copy.106 = bf16[2,40,8,1728]{3,1,2,0:T(8,128)(2,1)} copy(bf16[2,40,8,1728]{1,0,3,2:T(2,128)(2,1)} %bitcast.55) | data formatting | bytes 4423680 | tf_op jit(solution)/shard_map/all_to_all | solution.py:151
  424.7 3.2 copy-done
  428.0 6.1 %cache_pages.1 = bf16[16,2,128,384]{3,2,1,0:T(8,128)(2,1)} custom-call(s32[18]{0:T(128)S(1)} %pad_add_fusion.1.meta_ref, bf16[2,5120,384]{2,1,0:T(8,128)(2,1)S(1)} %copy-done), custom_call_target="tpu_custom_call" | custom-call | flops 10000000 | bytes 11000000 | tf_op jit(solution)/shard_map/cache_pages/pallas_call | solution.py:77
  434.1 4.5 multiply_reduce_fusion
  438.6 17.7 %psum.23 = f32[320]{0:T(512)S(1)} all-reduce(f32[320]{0:T(512)S(1)} %get-tuple-element.44), channel_id=1, replica_groups=mesh['row'=8,'col'=16] {'row'}, use_global_device_ids=true, to_apply=%region_8.9 | all-reduce | flops 320 | bytes 2560 | tf_op jit(solution)/shard_map/psum | solution.py:213
  456.3 2.0 add_convert_fusion
  (51 shorter events, 9.5 us)
Async XLA Ops:
  7.2 151.5 %all-gather.4.cloned.1.call-start = ((), (), s32[]{:S(2)}) async-start(), calls=%async_computation.5 | async-start | bytes 12533760 | tf_op jit(solution)/shard_map/all_gather | solution.py:164
  72.0 3.1 copy-start.5
  72.0 3.3 copy-start.3
  72.1 3.4 copy-start.6
  75.1 242.5 %all-gather.6.cloned.1.call-start = ((), (), s32[]{:S(2)}) async-start(), calls=%async_computation.6 | async-start | bytes 8355840 | tf_op jit(solution)/shard_map/all_gather | solution.py:190
  196.2 38.7 %all-to-all-start.3 = ((bf16[2,640,864]{2,0,1:T(2,128)(2,1)}), bf16[2,640,864]{2,0,1:T(2,128)(2,1)S(1)}, u32[]{:S(2)}, u32[]{:S(2)}) async-start(bf16[2,640,864]{2,0,1:T(2,128)(2,1)} %copy.94), calls=%async_computation.3 | async-start | bytes 4587520 | tf_op jit(solution)/shard_map/all_to_all | solution.py:152
  234.9 1.4 copy-start.1
  236.3 117.7 %all-to-all-start.2 = ((bf16[384,8,640]{0,2,1:T(8,128)(2,1)}), bf16[384,8,640]{0,2,1:T(8,128)(2,1)}, u32[]{:S(2)}, u32[]{:S(2)}) async-start(bf16[384,8,640]{0,2,1:T(8,128)(2,1)} %bitcast.56), calls=%async_computation.2 | async-start | bytes 7864320 | tf_op jit(solution)/shard_map/all_to_all | solution.py:210
  240.8 193.2 %all-gather.8.cloned.1.call-start = ((), (), s32[]{:S(2)}) async-start(), calls=%async_computation.7 | async-start | bytes 2211840 | tf_op jit(solution)/shard_map/all_gather | solution.py:211
  354.0 5.4 %copy-start.4 = (s32[4,16]{1,0:T(4,128)S(1)}, s32[4,16]{1,0:T(4,128)}, u32[]{:S(2)}) copy-start(s32[4,16]{1,0:T(4,128)} %param.12) | copy-start | bytes 772
  354.0 43.0 %all-to-all-start.4 = ((bf16[8,2,69120]{2,1,0:T(2,128)(2,1)}), bf16[8,2,69120]{2,1,0:T(2,128)(2,1)S(1)}, u32[]{:S(2)}, u32[]{:S(2)}) async-start(bf16[8,2,69120]{2,1,0:T(2,128)(2,1)} %reshape.170), calls=%async_computation.4 | async-start | bytes 4423680 | tf_op jit(solution)/shard_map/all_to_all | solution.py:151
  424.7 3.2 copy-start
  434.1 22.2 %copy-start.2 = (f32[640]{0:T(1024)S(1)}, f32[640]{0:T(1024)}, u32[]{:S(2)}) copy-start(f32[640]{0:T(1024)} %param.16) | copy-start | bytes 7684
Sparse Core Ops, SparseCore 0:
  75.2 83.3 all-gather.3
  188.8 128.8 all-gather.5
  327.3 71.1 all-gather.7
where the time goes:
time: 467 us; the launch traced here: 465 us
  waiting for transfers between devices  216 us (46%)
  local copies, waits for them, and re-layouts  99.1 us (21%)
  blocking collectives  81.7 us (17%)
  Pallas kernels  15.6 us (3%)
  between operations  13.9 us (3%)
  starting transfers between devices  13.7 us (3%)
  matrix products  13.5 us (3%)
  other arithmetic  11.7 us (3%)
    all_gather x1, waiting for transfers between devices, local(): shard_piece = lax.all_gather(weight_blocks, 'col', axis=2, tiled=True)  81.9 us
    all_gather x1, waiting for transfers between devices, local(): lax.all_gather(jnp.stack([key_rot, value_flat]), 'col', axis=1, tiled=True)  76.1 us
    unnamed x19, local copies, waits for them, and re-layouts  46.1 us
    all_to_all x1, waiting for transfers between devices, local(): lax.all_to_all(lax.all_to_all(trainer_gate_up, 'col', split_axis=1, conca...  29.3 us
    all_to_all x1, waiting for transfers between devices, local(): lax.all_to_all(trainer_gate_up, 'col', split_axis=1, concat_axis=2, tiled...  28.2 us
    all_to_all x1, blocking collectives, local(): lax.all_to_all(trainer_qkv, 'col', split_axis=1, concat_axis=2, tiled=True)  28.2 us
    psum x1, blocking collectives, local(): lax.psum((jnp.sum(query_rows * query_rows, axis=1), jnp.sum(key_rows * ke...  18.8 us
    psum x1, blocking collectives, local(): out_squares = lax.psum(jnp.sum(own_out * own_out, axis=1), 'row')  17.7 us
  transfers between devices with their start and end apart: 6, of which 4 were waited for; matrix products, arithmetic and copies ran while one was open for 17% of the time, Pallas kernels for 3%

commit v1 on v0

--- a/solution.py
+++ b/solution.py
@@ -127,6 +127,327 @@
     )(first, start, query, kv)
 
 
+def rdma(src, dst, send_sem, recv_sem, row, col):
+    return pltpu.make_async_remote_copy(
+        src_ref=src,
+        dst_ref=dst,
+        send_sem=send_sem,
+        recv_sem=recv_sem,
+        device_id=(row, col),
+        device_id_type=pl.DeviceIdType.MESH,
+    )
+
+
+def each(count, body):
+    lax.fori_loop(0, count, lambda i, carry: (body(i), carry)[1], 0)
+
+
+def signal(sem, row, col):
+    pl.semaphore_signal(sem, inc=1, device_id=(row, col), device_id_type=pl.DeviceIdType.MESH)
+
+
+def sync_body(
+    qkv_ref, gate_hbm, hid_ref, ow_hbm,
+    proj_ref, qblk_ref, gblk_ref, ocol_ref,
+    qsrc, qstage, w_all, gf32, gsrc, gstage,
+    q_send, q_recv, w_send, w_fwd, w_recv, g_send, g_recv, o_send, o_fwd, o_recv, local_sem,
+    *, n_row, n_col,
+):
+    row, col = lax.axis_index("row"), lax.axis_index("col")
+    chip, core = col // 2, lax.rem(col, 2)
+    chips = n_col // 2
+    half_rows = n_row // 2
+    step = qkv_ref.shape[1] // chips
+    fine = step // 2
+    sib = col + 1 - 2 * core
+    target_core = row // half_rows
+    self_row = chip == row
+
+    gate_copy = pltpu.make_async_copy(gate_hbm, gf32, local_sem.at[0])
+    gate_copy.start()
+
+    barrier = pltpu.get_barrier_semaphore()
+
+    def greet(i):
+        peer_row, peer_col = i // 2, 2 * row + lax.rem(i, 2)
+
+        @pl.when(jnp.logical_or(peer_row != row, peer_col != col))
+        def _():
+            signal(barrier, peer_row, peer_col)
+
+    each(2 * n_row, greet)
+    each(chips - 1, lambda i: signal(barrier, row, 2 * lax.rem(chip + 1 + i, chips) + core))
+    signal(barrier, row, sib)
+    each(n_row - 1, lambda i: signal(barrier, lax.rem(row + 1 + i, n_row), col))
+
+    for j in range(3):
+        qsrc[j] = qkv_ref[j].astype(jnp.bfloat16)
+    pl.semaphore_wait(barrier, n_col + (chips - 1) + 1 + (n_row - 1) - self_row.astype(jnp.int32))
+
+    def piece(to_chip):
+        return qsrc.at[:, pl.ds(pl.multiple_of(to_chip * step, 16), step), :]
+
+    def q_copy(i):
+        to_chip = lax.rem(chip + i, chips)
+        return rdma(
+            piece(to_chip), qstage.at[core, lax.rem(row, half_rows)],
+            q_send.at[i], q_recv.at[core, lax.rem(row, half_rows)],
+            chip, 2 * to_chip + target_core,
+        )
+
+    q_self = jnp.logical_and(self_row, target_core == core)
+    own_q = pltpu.make_async_copy(
+        piece(chip), qstage.at[core, lax.rem(row, half_rows)],
+        q_recv.at[core, lax.rem(row, half_rows)],
+    )
+
+    def q_start(i):
+        away = jnp.logical_or(i > 0, jnp.logical_not(q_self))
+
+        @pl.when(away)
+        def _():
+            q_copy(i).start()
+
+    each(chips, q_start)
+
+    @pl.when(q_self)
+    def _():
+        own_q.start()
+
+    gate_copy.wait()
+    for c in range(n_col):
+        for j in range(2):
+            gsrc[c, j] = gf32[j, c * fine:(c + 1) * fine, :].astype(jnp.bfloat16)
+
+    def q_wait(i):
+        half, src = lax.rem(i, 2), i // 2
+        rdma(
+            piece(0), qstage.at[half, src], q_send.at[0], q_recv.at[half, src], row, col
+        ).wait_recv()
+
+    each(2 * half_rows, q_wait)
+    width = w_all.shape[3]
+    place = pl.multiple_of(chip * step, 16)
+    for s in range(half_rows):
+        for j in range(3):
+            both = jnp.concatenate(
+                [qstage[0, s, j].astype(jnp.float32), qstage[1, s, j].astype(jnp.float32)], axis=1
+            )
+            w_all[j, core * half_rows + s, pl.ds(place, step), :] = both.astype(jnp.bfloat16)
+
+    def block(of_chip, of_core):
+        return w_all.at[
+            :, pl.ds(of_core * half_rows, half_rows),
+            pl.ds(pl.multiple_of(of_chip * step, 16), step), :
+        ]
+
+    def w_copy(i):
+        to_chip = lax.rem(chip + 1 + i, chips)
+        return rdma(
+            block(chip, core), block(chip, core),
+            w_send.at[i], w_recv.at[chip, core], row, 2 * to_chip + core,
+        )
+
+    def w_forward(of_chip):
+        return rdma(
+            block(of_chip, core), block(of_chip, core),
+            w_fwd.at[of_chip], w_recv.at[of_chip, core], row, sib,
+        )
+
+    def w_arrived(of_chip, of_core):
+        rdma(
+            block(of_chip, of_core), block(of_chip, of_core),
+            w_send.at[0], w_recv.at[of_chip, of_core], row, col,
+        ).wait_recv()
+
+    each(chips - 1, lambda i: w_copy(i).start())
+    w_forward(chip).start()
+
+    def g_copy(i):
+        to_col = lax.rem(col + i, n_col)
+        return rdma(
+            gsrc.at[to_col], gstage.at[core, row], g_send.at[i], g_recv.at[core, row], chip, to_col
+        )
+
+    own_g = pltpu.make_async_copy(gsrc.at[col], gstage.at[core, row], g_recv.at[core, row])
+
+    def g_start(i):
+        @pl.when(jnp.logical_or(i > 0, jnp.logical_not(self_row)))
+        def _():
+            g_copy(i).start()
+
+    each(n_col, g_start)
+
+    @pl.when(self_row)
+    def _():
+        own_g.start()
+
+    own_rows = ow_hbm.shape[0]
+    half_o = own_rows // 2
+    out_width = ocol_ref.shape[1]
+
+    def o_src(of_core, to_row):
+        return ow_hbm.at[
+            pl.ds(pl.multiple_of(of_core * half_o, 16), half_o),
+            pl.ds(pl.multiple_of(to_row * out_width, 128), out_width),
+        ]
+
+    def o_dst(of_row, of_core):
+        return ocol_ref.at[
+            pl.ds(pl.multiple_of(of_row * own_rows + of_core * half_o, 16), half_o), :
+        ]
+
+    def o_copy(i):
+        to_row = lax.rem(row + 1 + i, n_row)
+        return rdma(
+            o_src(core, to_row), o_dst(row, core), o_send.at[i], o_recv.at[row, core], to_row, col
+        )
+
+    def o_forward(of_row):
+        return rdma(
+            o_dst(of_row, core), o_dst(of_row, core),
+            o_fwd.at[of_row], o_recv.at[of_row, core], row, sib,
+        )
+
+    def o_arrived(of_row, of_core):
+        rdma(
+            o_dst(of_row, of_core), o_dst(of_row, of_core),
+            o_send.at[0], o_recv.at[of_row, of_core], row, col,
+        ).wait_recv()
+
+    own_o = pltpu.make_async_copy(
+        ow_hbm.at[:, pl.ds(pl.multiple_of(row * out_width, 128), out_width)],
+        ocol_ref.at[pl.ds(pl.multiple_of(row * own_rows, 16), own_rows), :],
+        local_sem.at[1],
+    )
+    each(n_row - 1, lambda i: o_copy(i).start())
+    own_o.start()
+
+    def w_relay(i):
+        of_chip = lax.rem(chip + chips - 1 - i, chips)
+        w_arrived(of_chip, core)
+        w_forward(of_chip).start()
+
+    each(chips - 1, w_relay)
+
+    def o_relay(i):
+        of_row = lax.rem(row + n_row - 1 - i, n_row)
+        o_arrived(of_row, core)
+        o_forward(of_row).start()
+
+    each(n_row - 1, o_relay)
+    each(chips, lambda i: w_arrived(lax.rem(chip + chips - i, chips), 1 - core))
+
+    row_width = w_all.shape[2]
+    for j in range(3):
+        proj_ref[j] = jnp.zeros_like(proj_ref[j])
+
+    def project(r):
+        lanes = pl.ds(pl.multiple_of(r * row_width, 128), row_width)
+        for j in range(3):
+            proj_ref[j] += jnp.dot(
+                hid_ref[:, lanes], w_all[j, r], preferred_element_type=jnp.float32
+            )
+
+    each(n_row, project)
+
+    def own_rows_of(r):
+        for j in range(3):
+            rows = w_all[j, r, pl.ds(place, step), :].astype(jnp.float32)
+            rows = jnp.where(core == 0, rows[:fine], rows[fine:])
+            qblk_ref[j, r] = rows.astype(jnp.bfloat16)
+
+    each(n_row, own_rows_of)
+
+    def g_wait(i):
+        half, src = lax.rem(i, 2), i // 2
+        rdma(
+            gsrc.at[0], gstage.at[half, src], g_send.at[0], g_recv.at[half, src], row, col
+        ).wait_recv()
+
+    each(2 * n_row, g_wait)
+
+    def g_join(r):
+        for j in range(2):
+            both = jnp.concatenate(
+                [gstage[0, r, j].astype(jnp.float32), gstage[1, r, j].astype(jnp.float32)], axis=1
+            )
+            gblk_ref[j, r] = both.astype(jnp.bfloat16)
+
+    each(n_row, g_join)
+
+    each(n_row - 1, lambda i: o_arrived(lax.rem(row + 1 + i, n_row), 1 - core))
+    own_o.wait()
+
+    def q_done(i):
+        @pl.when(jnp.logical_or(i > 0, jnp.logical_not(q_self)))
+        def _():
+            q_copy(i).wait_send()
+
+    def g_done(i):
+        @pl.when(jnp.logical_or(i > 0, jnp.logical_not(self_row)))
+        def _():
+            g_copy(i).wait_send()
+
+    each(chips, q_done)
+    each(n_col, g_done)
+    each(chips - 1, lambda i: w_copy(i).wait_send())
+    each(chips, lambda i: w_forward(i).wait_send())
+    each(n_row - 1, lambda i: o_copy(i).wait_send())
+    each(n_row - 1, lambda i: o_forward(lax.rem(row + 1 + i, n_row)).wait_send())
+
+
+def sync_weights(qkv_train, gate_up_train, hidden, o_weight, n_row, n_col):
+    tok, width_model = hidden.shape
+    row_width, part = qkv_train.shape[1:]
+    gate_part = gate_up_train.shape[2]
+    width = 2 * part
+    chips = n_col // 2
+    half_rows = n_row // 2
+    step = row_width // chips
+    fine = step // 2
+    bf16, f32 = jnp.bfloat16, jnp.float32
+    dma = pltpu.SemaphoreType.DMA
+    vmem, anywhere = pl.BlockSpec(memory_space=pltpu.VMEM), pl.BlockSpec(memory_space=pl.ANY)
+    return pl.pallas_call(
+        functools.partial(sync_body, n_row=n_row, n_col=n_col),
+        out_shape=(
+            jax.ShapeDtypeStruct((3, tok, width), f32),
+            jax.ShapeDtypeStruct((3, n_row, fine, width), bf16),
+            jax.ShapeDtypeStruct((2, n_row, fine, 2 * gate_part), bf16),
+            jax.ShapeDtypeStruct((n_row * o_weight.shape[0], width_model // n_row), bf16),
+        ),
+        in_specs=[vmem, anywhere, vmem, anywhere],
+        out_specs=(vmem, vmem, vmem, anywhere),
+        scratch_shapes=[
+            pltpu.VMEM((3, row_width, part), bf16),
+            pltpu.VMEM((2, half_rows, 3, step, part), bf16),
+            pltpu.VMEM((3, n_row, row_width, width), bf16),
+            pltpu.VMEM((2, row_width, gate_part), f32),
+            pltpu.VMEM((n_col, 2, fine, gate_part), bf16),
+            pltpu.VMEM((2, n_row, 2, fine, gate_part), bf16),
+            dma((chips,)),
+            dma((2, half_rows)),
+            dma((chips,)),
+            dma((chips,)),
+            dma((chips, 2)),
+            dma((n_col,)),
+            dma((2, n_row)),
+            dma((n_row,)),
+            dma((n_row,)),
+            dma((n_row, 2)),
+            dma((2,)),
+        ],
+        compiler_params=pltpu.CompilerParams(
+            collective_id=1, has_side_effects=True, vmem_limit_bytes=60 << 20
+        ),
+        cost_estimate=pl.CostEstimate(
+            flops=2 * 3 * tok * width_model * width, bytes_accessed=30_000_000, transcendentals=0
+        ),
+        name="sync_weights",
+    )(qkv_train, gate_up_train, hidden, o_weight)
+
+
 def local(
     hidden, lengths, owner, page_table, qkv_train, qk_gain, o_weight, post_gain, gate_up_train
 ):
@@ -138,37 +459,14 @@
     model_width = hidden.shape[1]
     row_width = model_width // n_row
     col_block = row_width // n_col
-    trainer_qkv = qkv_train.astype(jnp.bfloat16)
-    trainer_gate_up = gate_up_train.astype(jnp.bfloat16)
-    server_qkv, server_gate_up = (
-        lax.all_to_all(
-            lax.all_to_all(trainer_qkv, "col", split_axis=1, concat_axis=2, tiled=True),
-            "row",
-            split_axis=2,
-            concat_axis=1,
-            tiled=True,
-        ),
-        lax.all_to_all(
-            lax.all_to_all(trainer_gate_up, "col", split_axis=1, concat_axis=2, tiled=True),
-            "row",
-            split_axis=2,
-            concat_axis=1,
-            tiled=True,
-        ),
-    )
-    heads_width = server_qkv.shape[2]
+    projected, weight_blocks, gate_up_blocks, o_columns = sync_weights(
+        qkv_train, gate_up_train, hidden, o_weight, n_row, n_col
+    )
+    heads_width = projected.shape[2]
     local_heads = heads_width // HD
-    weight_blocks = server_qkv.reshape(3, n_row, col_block, heads_width)
-    gate_up_blocks = server_gate_up.reshape(2, n_row, col_block, server_gate_up.shape[2])
-    hidden_three = hidden.reshape(tok_rows, n_row, row_width)
-    shard_piece = lax.all_gather(weight_blocks, "col", axis=2, tiled=True)
-    shards = shard_piece.shape[2] // col_block
-    projected = jnp.einsum(
-        "trb,jrbh->tjh", hidden_three, shard_piece, preferred_element_type=jnp.float32
-    )
-    query_rows = projected[:, 0]
-    key_rows = projected[:, 1]
-    value_rows = projected[:, 2]
+    query_rows = projected[0]
+    key_rows = projected[1]
+    value_rows = projected[2]
     query_squares, key_squares = lax.psum(
         (jnp.sum(query_rows * query_rows, axis=1), jnp.sum(key_rows * key_rows, axis=1)), "row"
     )
@@ -207,7 +505,6 @@
     first = jnp.stack([col_index * tok_rows, first_key]).astype(jnp.int32)
     attention = attend(first, token_start[:, None], query_rot, kv, span)
 
-    o_columns = lax.all_to_all(o_weight, "row", split_axis=1, concat_axis=0, tiled=True)
     attention_all = lax.all_gather(attention, "row", axis=1, tiled=True)
     own_out = jnp.dot(attention_all, o_columns, preferred_element_type=jnp.float32)
     out_squares = lax.psum(jnp.sum(own_out * own_out, axis=1), "row")

time: 467 us -> 432 us (0.925)
  Pallas kernels: 15.6 us -> 214 us
  waiting for transfers between devices: 216 us -> 123 us
  local copies, waits for them, and re-layouts: 99.1 us -> 17.3 us
  blocking collectives: 81.7 us -> 49 us
  starting transfers between devices: 13.7 us -> 0.26 us
  matrix products: 13.5 us -> 4.49 us
    pallas_call x0 -> x1, Pallas kernels: none -> 198 us  [sync_weights(): pl.pallas_call(functools.partial(sync_body, n_row=n_row, n_col=n_col), ou...]
    all_gather x1 -> x0, waiting for transfers between devices: 81.9 us -> none  [local(): shard_piece = lax.all_gather(weight_blocks, 'col', axis=2, tiled=True)]
    all_to_all x3 -> x0, waiting for transfers between devices: 57.5 us -> none  [the longest x1 29.3 us: local(): lax.all_to_all(lax.all_to_all(trainer_gate_up, 'col', split_axis=1, conca...]
    all_to_all x7 -> x0, local copies, waits for them, and re-layouts: 45.6 us -> none  [the longest x1 15.7 us: local(): lax.all_to_all(lax.all_to_all(trainer_gate_up, 'col', split_axis=1, conca...]
    all_to_all x2 -> x0, blocking collectives: 45.2 us -> none  [the longest x1 28.2 us: local(): lax.all_to_all(trainer_qkv, 'col', split_axis=1, concat_axis=2, tiled=True)]
    all_gather x1, waiting for transfers between devices: 0.01 us -> 36 us  [local(): attention_all = lax.all_gather(attention, 'row', axis=1, tiled=True)]
    unnamed x19 -> x18, local copies, waits for them, and re-layouts: 46.1 us -> 15.3 us
    all_to_all x3 -> x0, starting transfers between devices: 13.4 us -> none  [the longest x1 4.71 us: local(): lax.all_to_all(lax.all_to_all(trainer_gate_up, 'col', split_axis=1, conca...]
  transfers between devices with their start and end apart: 6 -> 2, of which waited for: 4 -> 2; matrix products, arithmetic and copies ran while one was open for 17% -> 1% of each run, Pallas kernels for 3% -> 1%
where the time goes in v1:
time: 432 us; the launch traced here: 431 us
  Pallas kernels  214 us (50%)
  waiting for transfers between devices  123 us (28%)
  blocking collectives  49 us (11%)
  local copies, waits for them, and re-layouts  17.3 us (4%)
  between operations  14.2 us (3%)
  other arithmetic  9.05 us (2%)
  matrix products  4.49 us (1%)
    pallas_call x1, Pallas kernels, sync_weights(): pl.pallas_call(functools.partial(sync_body, n_row=n_row, n_col=n_col), ou...  198 us
    all_gather x1, waiting for transfers between devices, local(): lax.all_gather(jnp.stack([key_rot, value_flat]), 'col', axis=1, tiled=True)  87.4 us
    all_gather x1, waiting for transfers between devices, local(): attention_all = lax.all_gather(attention, 'row', axis=1, tiled=True)  36 us
    psum x1, blocking collectives, local(): lax.psum((jnp.sum(query_rows * query_rows, axis=1), jnp.sum(key_rows * ke...  31.1 us
    psum x1, blocking collectives, local(): out_squares = lax.psum(jnp.sum(own_out * own_out, axis=1), 'row')  17.9 us
    unnamed x18, local copies, waits for them, and re-layouts  15.3 us
    pallas_call x1, Pallas kernels, attend(): pl.pallas_call(functools.partial(attend_body, span=span), out_shape=jax.S...  9.46 us
  transfers between devices with their start and end apart: 2, of which 2 were waited for; matrix products, arithmetic and copies ran while one was open for 1% of the time, Pallas kernels for 1%

profile of v1, /device:TPU:0, one launch (start us, length us, event | category | flops | bytes accessed | tf_op | source)
XLA Modules:
  0.0 431.5 jit_solution(17974464608932422297)
XLA Ops:
  7.2 2.8 copy.22.qkv_ref
  10.1 5.7 %copy.23.gate_hbm = f32[2,640,864]{2,1,0:T(8,128)} copy(f32[2,640,864]{1,2,0:T(8,128)} %param.17) | data formatting | bytes 8847360 | tf_op args[8]
  15.8 198.1 %sync_weights.1 = (f32[3,320,384]{2,1,0:T(8,128)}, bf16[3,8,40,384]{3,2,1,0:T(8,128)(2,1)}, bf16[2,8,40,1728]{3,2,1,0:T(8,128)(2,1)}, bf16[3072,640]{1,0:T(8,128)(2,1)}) custom-call(f32[3,640,192]{2,1,0:T(8,128)} %copy.22.qkv_ref, f32[2,640,864]{2,1,0:T(8,128)} %copy.23.gate_hbm, bf16[320,5120]{1,0:T(8,128)(2,1)} %hid_ref.1, bf16[384,5120]{1,0:T(8,128)(2,1)} %ow_hbm.1), custom_call_target="tpu_custom_call" | custom-call | flops 3774873600 | bytes 30000000 | tf_op jit(solution)/shard_map/sync_weights/pallas_call | solution.py:412
  214.0 1.4 multiply_reduce_fusion.1
  215.4 1.1 slice.55
  216.5 0.2 copy.25
  216.7 0.2 reduce-window.8
  216.9 0.7 select_reduce_fusion.3
  217.8 0.2 copy.24
  218.0 31.1 %all-reduce = (f32[320]{0:T(512)S(1)}, f32[320]{0:T(512)S(1)}) all-reduce(f32[320]{0:T(512)S(1)} %get-tuple-element.13, f32[320]{0:T(512)S(1)} %get-tuple-element.12), channel_id=1, replica_groups=mesh['row'=8,'col'=16] {'row'}, use_global_device_ids=true, to_apply=%region_4.0 | all-reduce | flops 640 | bytes 5120 | tf_op jit(solution)/shard_map/psum | solution.py:470
  249.1 0.4 multiply_cosine_fusion
  249.6 0.1 multiply_multiply_fusion
  249.7 0.1 multiply_multiply_fusion.1
  249.8 0.2 subtract_convert_fusion
  250.0 0.2 copy.26
  250.2 0.8 pad_maximum_fusion
  251.1 0.2 all-gather.5.cloned.1.call-start
  251.3 0.1 broadcast_in_dim.60.start_ref
  251.5 0.2 copy.28.query_ref
  251.8 87.4 %all-gather.3.cloned.1.call-done.kv_ref = bf16[2,5120,384]{2,1,0:T(8,128)(2,1)} async-done(((bf16[2,320,384]{2,1,0:T(8,128)(2,1)}), bf16[2,5120,384]{2,1,0:T(8,128)(2,1)}) %all-gather.3.cloned.1.call-update) | async-done | bytes 7864336 | tf_op jit(solution)/shard_map/all_gather | solution.py:488
  339.2 9.5 %attend.1 = bf16[320,384]{1,0:T(8,128)(2,1)} custom-call(s32[2]{0:T(128)S(1)} %pad_add_fusion.first_ref, s32[320,1]{1,0:T(8,128)S(1)} %broadcast_in_dim.60.start_ref, bf16[320,384]{1,0:T(8,128)(2,1)S(1)} %copy.28.query_ref, bf16[2,5120,384]{2,1,0:T(8,128)(2,1)} %all-gather.3.cloned.1.call-done.kv_ref), custom_call_target="tpu_custom_call" | custom-call | flops 1258291200 | bytes 8000000 | tf_op jit(solution)/shard_map/attend/pallas_call | solution.py:114
  348.7 0.6 reduce_or.9
  349.4 0.6 broadcast_select_fusion
  350.0 1.4 pad_add_fusion.1.meta_ref
  351.5 3.2 copy-done
  354.7 6.1 %cache_pages.1 = bf16[16,2,128,384]{3,2,1,0:T(8,128)(2,1)} custom-call(s32[18]{0:T(128)S(1)} %pad_add_fusion.1.meta_ref, bf16[2,5120,384]{2,1,0:T(8,128)(2,1)S(1)} %copy-done), custom_call_target="tpu_custom_call" | custom-call | flops 10000000 | bytes 11000000 | tf_op jit(solution)/shard_map/cache_pages/pallas_call | solution.py:77
  360.8 36.0 %all-gather.5.cloned.1.call-done = bf16[320,3072]{1,0:T(8,128)(2,1)} async-done(((bf16[320,384]{1,0:T(8,128)(2,1)}), bf16[320,3072]{1,0:T(8,128)(2,1)}) %all-gather.5.cloned.1.call-update) | async-done | bytes 1966096 | tf_op jit(solution)/shard_map/all_gather | solution.py:508
  396.8 4.5 %multiply_reduce_fusion = (f32[320]{0:T(512)S(1)}, f32[320,640]{1,0:T(8,128)S(1)}) fusion(bf16[320,3072]{1,0:T(8,128)(2,1)} %all-gather.5.cloned.1.call-done, bf16[3072,640]{1,0:T(8,128)(2,1)} %get-tuple-element.9), kind=kOutput, calls=%fused_computation.1 | convolution fusion | flops 1258700544 | bytes 6718720 | tf_op jit(solution)/shard_map/dot_general | solution.py:509
  401.3 17.9 %psum.23 = f32[320]{0:T(512)S(1)} all-reduce(f32[320]{0:T(512)S(1)} %get-tuple-element.32), channel_id=1, replica_groups=mesh['row'=8,'col'=16] {'row'}, use_global_device_ids=true, to_apply=%region_8.9 | all-reduce | flops 320 | bytes 2560 | tf_op jit(solution)/shard_map/psum | solution.py:510
  419.2 2.0 add_convert_fusion
  421.2 2.1 copy.31
  423.2 1.4 copy.32
  (28 shorter events, 0.6 us)
Async XLA Ops:
  7.2 332.0 %all-gather.3.cloned.1.call-start = ((), (), s32[]{:S(2)}) async-start(), calls=%async_computation | async-start | bytes 8355840 | tf_op jit(solution)/shard_map/all_gather | solution.py:488
  213.9 2.8 copy-start.3
  213.9 2.8 copy-start.5
  214.0 3.0 copy-start.6
  251.1 145.7 %all-gather.5.cloned.1.call-start = ((), (), s32[]{:S(2)}) async-start(), calls=%async_computation.1 | async-start | bytes 2211840 | tf_op jit(solution)/shard_map/all_gather | solution.py:508
  251.8 97.5 %copy-start.4 = (s32[4,16]{1,0:T(4,128)S(1)}, s32[4,16]{1,0:T(4,128)}, u32[]{:S(2)}) copy-start(s32[4,16]{1,0:T(4,128)} %param.12) | copy-start | bytes 772
  351.5 3.2 copy-start
  396.8 22.4 %copy-start.2 = (f32[640]{0:T(1024)S(1)}, f32[640]{0:T(1024)}, u32[]{:S(2)}) copy-start(f32[640]{0:T(1024)} %param.16) | copy-start | bytes 7684
  401.3 21.9 %copy-start.1 = (bf16[2,8,40,1728]{3,2,1,0:T(8,128)(2,1)S(1)}, bf16[2,8,40,1728]{3,2,1,0:T(8,128)(2,1)}, u32[]{:S(2)}) copy-start(bf16[2,8,40,1728]{3,2,1,0:T(8,128)(2,1)} %get-tuple-element.43) | copy-start | bytes 6635524
Sparse Core Ops, SparseCore 0:
  251.2 87.8 all-gather.2
  348.8 47.9 all-gather.4

commit v2 on v0

--- a/solution.py
+++ b/solution.py
@@ -127,6 +127,411 @@
     )(first, start, query, kv)
 
 
+def rdma(src, dst, send_sem, recv_sem, device):
+    return pltpu.make_async_remote_copy(
+        src_ref=src,
+        dst_ref=dst,
+        send_sem=send_sem,
+        recv_sem=recv_sem,
+        device_id=device,
+        device_id_type=pl.DeviceIdType.MESH,
+    )
+
+
+def arrived(ref, recv_sem, send_sem, here):
+    rdma(ref, ref, send_sem, recv_sem, here).wait_recv()
+
+
+def each(count, body):
+    lax.fori_loop(0, count, lambda i, carry: (body(i), carry)[1], 0)
+
+
+def wrap(value, size):
+    return lax.rem(value + size, size)
+
+
+class Place:
+    def __init__(self):
+        self.row, self.col = lax.axis_index("row"), lax.axis_index("col")
+        self.y, self.zl = self.row // 2, lax.rem(self.row, 2)
+        self.zh, self.x, self.core = self.col // 8, lax.rem(self.col // 2, 4), lax.rem(self.col, 2)
+        self.chip = self.col // 2
+        self.here = (self.row, self.col)
+
+    def at(self, y=None, zl=None, zh=None, x=None, core=None):
+        y, zl = (self.y if y is None else y), (self.zl if zl is None else zl)
+        zh, x = (self.zh if zh is None else zh), (self.x if x is None else x)
+        core = self.core if core is None else core
+        return (2 * y + zl, 8 * zh + 2 * x + core)
+
+
+def signal(sem, device):
+    pl.semaphore_signal(sem, inc=1, device_id=device, device_id_type=pl.DeviceIdType.MESH)
+
+
+class Relay:
+    def __init__(self, me, src, stages, send, recv):
+        self.me, self.src, self.stages, self.send, self.recv = me, src, stages, send, recv
+
+    def go(self, away, stage, number, slot, src, device):
+        dst, recv = self.stages[stage].at[slot], self.recv.at[stage, slot]
+
+        @pl.when(away)
+        def _():
+            rdma(src, dst, self.send.at[stage, number], recv, device).start()
+
+        @pl.when(jnp.logical_not(away))
+        def _():
+            pltpu.make_async_copy(src, dst, recv).start()
+
+    def got(self, stage, slot):
+        arrived(
+            self.stages[stage].at[slot], self.recv.at[stage, slot], self.send.at[stage, 0],
+            self.me.here,
+        )
+
+    def first(self):
+        me = self.me
+
+        def send(i):
+            dx, dk, zh = i // 4, lax.rem(i // 2, 2), lax.rem(i, 2)
+            x, core = lax.rem(me.x + dx, 4), lax.rem(me.core + dk, 2)
+            device = me.at(x=x, core=core)
+            slot = (me.x * 2 + me.core) * 2 + zh
+            self.go(i >= 2, 0, i, slot, self.src.at[zh * 8 + 2 * x + core], device)
+
+        each(16, send)
+
+    def second(self):
+        me = self.me
+
+        def send(i):
+            dx, ks, zh = i // 4, lax.rem(i // 2, 2), lax.rem(i, 2)
+            xs = wrap(me.x - dx, 4)
+            came = (xs * 2 + ks) * 2 + zh
+            self.got(0, came)
+            zl = lax.rem(xs, 2)
+            away = jnp.logical_or(zl != me.zl, zh != me.zh)
+            slot = ((me.zh * 2 + me.zl) * 2 + xs // 2) * 2 + ks
+            self.go(away, 1, came, slot, self.stages[0].at[came], me.at(zl=zl, zh=zh))
+
+        each(16, send)
+
+    def third(self):
+        me = self.me
+
+        def send(i):
+            zs = lax.rem(me.zh * 2 + me.zl + i // 4, 4)
+            xh, ks = lax.rem(i // 2, 2), lax.rem(i, 2)
+            came = (zs * 2 + xh) * 2 + ks
+            self.got(1, came)
+            y = (zs // 2) * 2 + xh
+            slot = ks * 8 + me.y * 2 + lax.rem(zs, 2)
+            self.go(y != me.y, 2, came, slot, self.stages[1].at[came], me.at(y=y))
+
+        each(16, send)
+
+    def last(self):
+        each(16, lambda i: self.got(2, i))
+
+    def drain(self):
+        me = self.me
+
+        def sent(away, stage, number):
+            @pl.when(away)
+            def _():
+                rdma(
+                    self.src.at[0], self.src.at[0], self.send.at[stage, number],
+                    self.recv.at[stage, 0], me.here,
+                ).wait_send()
+
+        def each_piece(i):
+            sent(i >= 2, 0, i)
+            xs, zh = i // 4, lax.rem(i, 2)
+            sent(jnp.logical_or(lax.rem(xs, 2) != me.zl, zh != me.zh), 1, i)
+            zs, xh = i // 4, lax.rem(i // 2, 2)
+            sent((zs // 2) * 2 + xh != me.y, 2, i)
+
+        each(16, each_piece)
+
+
+class ColGather:
+    def __init__(self, me, view, send, recv):
+        self.me, self.view, self.send, self.recv = me, view, send, recv
+        self.sent = []
+
+    def chip(self, dz, dx):
+        return wrap(self.me.zh + dz, 2) * 4 + wrap(self.me.x + dx, 4)
+
+    def copy(self, chip, half, kind):
+        me = self.me
+        device = [
+            me.at(x=wrap(me.x + 1, 4)), me.at(x=wrap(me.x - 1, 4)), me.at(zh=1 - me.zh),
+            me.at(core=1 - me.core),
+        ][kind]
+        ref = self.view(chip, me.core, half)
+        return rdma(
+            ref, ref, self.send.at[chip, half, kind], self.recv.at[chip, me.core, half], device
+        )
+
+    def go(self, chip, half, *kinds):
+        for kind in kinds:
+            self.copy(chip, half, kind).start()
+            self.sent.append((chip, half, kind))
+
+    def got(self, chip, core, half):
+        arrived(
+            self.view(chip, core, half), self.recv.at[chip, core, half], self.send.at[0, 0, 0],
+            self.me.here,
+        )
+
+    def start(self):
+        for half in range(2):
+            self.go(self.chip(0, 0), half, 2, 0, 1, 3)
+
+    def z_turn(self):
+        for half in range(2):
+            self.got(self.chip(1, 0), self.me.core, half)
+            self.go(self.chip(1, 0), half, 0, 1, 3)
+
+    def x_turn(self, dz, *more):
+        left, right = self.chip(dz, -1), self.chip(dz, 1)
+        core = self.me.core
+        self.got(left, core, 0)
+        self.go(left, 0, 0, *more, 3)
+        self.got(right, core, 1)
+        self.go(right, 1, 1, *more, 3)
+        self.got(left, core, 1)
+        self.go(left, 1, *more, 3)
+        self.got(right, core, 0)
+        self.go(right, 0, *more, 3)
+
+    def x_end(self, dz, *more):
+        for half in range(2):
+            self.got(self.chip(dz, 2), self.me.core, half)
+            self.go(self.chip(dz, 2), half, *more, 3)
+
+    def z_end(self):
+        for dx in (0, -1, 1, 2):
+            for half in range(2):
+                self.got(self.chip(1, dx), self.me.core, half)
+                self.go(self.chip(1, dx), half, 3)
+
+    def sibling(self, dz, dx):
+        for half in range(2):
+            self.got(self.chip(dz, dx), 1 - self.me.core, half)
+
+    def drain(self):
+        for which in self.sent:
+            self.copy(*which).wait_send()
+        self.sent = []
+
+
+def sync_body(
+    qkv_ref, gate_hbm, hid_ref, ow_hbm,
+    proj_ref, qblk_ref, gblk_ref, ocol_ref,
+    hid_parts, qsrc, q1, q2, q3, w_all, gf32, gsrc, g1, g2, g3,
+    q_send, q_recv, g_send, g_recv, w_send, w_recv, o_send, o_fwd, o_recv, local_sem,
+    *, n_row, n_col,
+):
+    me = Place()
+    row, col, core = me.row, me.col, me.core
+    width_row = qkv_ref.shape[2]
+    fine = width_row // n_col
+    bf16, f32 = jnp.bfloat16, jnp.float32
+
+    def fetch(j):
+        return pltpu.make_async_copy(gate_hbm.at[j], gf32.at[j], local_sem.at[j])
+
+    for j in range(2):
+        fetch(j).start()
+
+    barrier = pltpu.get_barrier_semaphore()
+    for i in range(1, 8):
+        signal(barrier, me.at(x=lax.rem(me.x + i // 2, 4), core=lax.rem(me.core + i, 2)))
+    for i in range(1, 4):
+        signal(barrier, me.at(zh=lax.rem(me.zh + i // 2, 2), zl=lax.rem(me.zl + i, 2)))
+    for i in range(1, n_row):
+        signal(barrier, (lax.rem(row + i, n_row), col))
+
+    for j in range(3):
+        turned = qkv_ref[j].T
+        for c in range(n_col):
+            qsrc[c, j] = turned[c * fine:(c + 1) * fine, :].astype(bf16)
+    pl.semaphore_wait(barrier, 7 + 3 + n_row - 1)
+
+    qkv = Relay(me, qsrc, (q1, q2, q3), q_send, q_recv)
+    gate = Relay(me, gsrc, (g1, g2, g3), g_send, g_recv)
+    qkv.first()
+    for j in range(2):
+        fetch(j).wait()
+        turned = gf32[j].T
+        for c in range(n_col):
+            gsrc[c, j] = turned[c * fine:(c + 1) * fine, :].astype(bf16)
+    qkv.second()
+    gate.first()
+    qkv.third()
+    qkv.last()
+
+    def join(stage, r, j):
+        return jnp.concatenate(
+            [stage[r, j].astype(f32), stage[n_row + r, j].astype(f32)], axis=1
+        )
+
+    for j in range(3):
+        for pair in range(n_row // 2):
+            first, second = join(q3, 2 * pair, j), join(q3, 2 * pair + 1, j)
+            qblk_ref[j, 2 * pair] = first.astype(bf16)
+            qblk_ref[j, 2 * pair + 1] = second.astype(bf16)
+            both = jnp.concatenate([first, second], axis=0).astype(bf16)
+            w_all[me.chip, core, j, pair * 2 * fine:(pair + 1) * 2 * fine, :] = both
+
+    depth = w_all.shape[3] // 2
+    weights = ColGather(me, lambda p, k, h: w_all.at[p, k, :, h * depth:(h + 1) * depth, :], w_send, w_recv)
+    weights.start()
+
+    own_rows = ow_hbm.shape[0]
+    half_o = own_rows // 2
+    out_width = ocol_ref.shape[1]
+
+    def o_src(to_row):
+        return ow_hbm.at[
+            pl.ds(pl.multiple_of(core * half_o, 16), half_o),
+            pl.ds(pl.multiple_of(to_row * out_width, 128), out_width),
+        ]
+
+    def o_dst(of_row, of_core):
+        return ocol_ref.at[
+            pl.ds(pl.multiple_of(of_row * own_rows + of_core * half_o, 16), half_o), :
+        ]
+
+    def o_copy(i):
+        to_row = lax.rem(row + 1 + i, n_row)
+        return rdma(
+            o_src(to_row), o_dst(row, core), o_send.at[i], o_recv.at[row, core], (to_row, col)
+        )
+
+    def o_forward(of_row):
+        return rdma(
+            o_dst(of_row, core), o_dst(of_row, core), o_fwd.at[of_row], o_recv.at[of_row, core],
+            me.at(core=1 - core),
+        )
+
+    def o_arrived(of_row, of_core):
+        arrived(o_dst(of_row, of_core), o_recv.at[of_row, of_core], o_send.at[0], me.here)
+
+    own_o = pltpu.make_async_copy(
+        ow_hbm.at[:, pl.ds(pl.multiple_of(row * out_width, 128), out_width)],
+        ocol_ref.at[pl.ds(pl.multiple_of(row * own_rows, 16), own_rows), :],
+        local_sem.at[2],
+    )
+    own_o.start()
+
+    def part(c):
+        return jnp.concatenate(
+            [
+                hid_ref[:, r * width_row + c * fine:r * width_row + (c + 1) * fine].astype(f32)
+                for r in range(n_row)
+            ],
+            axis=1,
+        ).astype(bf16)
+
+    for c in range(n_col):
+        hid_parts[c] = part(c)
+
+    gate.second()
+    weights.z_turn()
+    each(n_row - 1, lambda i: o_copy(i).start())
+    weights.x_turn(0)
+    weights.x_turn(1)
+    gate.third()
+    weights.x_end(0)
+    weights.x_end(1)
+
+    for j in range(3):
+        proj_ref[j] = jnp.zeros_like(proj_ref[j])
+
+    def project(chip, of_core):
+        lhs = hid_parts[2 * chip + of_core]
+        for j in range(3):
+            proj_ref[j] += jnp.dot(lhs, w_all[chip, of_core, j], preferred_element_type=f32)
+
+    each(n_col // 2, lambda chip: project(chip, core))
+    for dz in range(2):
+        for dx in (0, -1, 1, 2):
+            weights.sibling(dz, dx)
+    each(n_col // 2, lambda chip: project(chip, 1 - core))
+
+    def o_relay(i):
+        of_row = lax.rem(row + n_row - 1 - i, n_row)
+        o_arrived(of_row, core)
+        o_forward(of_row).start()
+
+    each(n_row - 1, o_relay)
+    gate.last()
+
+    def g_join(r):
+        for j in range(2):
+            gblk_ref[j, r] = join(g3, r, j).astype(bf16)
+
+    each(n_row, g_join)
+    each(n_row - 1, lambda i: o_arrived(lax.rem(row + 1 + i, n_row), 1 - core))
+    own_o.wait()
+    qkv.drain()
+    gate.drain()
+    weights.drain()
+    each(n_row - 1, lambda i: o_copy(i).wait_send())
+    each(n_row - 1, lambda i: o_forward(lax.rem(row + 1 + i, n_row)).wait_send())
+
+
+def sync_weights(qkv_train, gate_up_train, hidden, o_weight, n_row, n_col):
+    tok, width_model = hidden.shape
+    row_width, part = qkv_train.shape[1:]
+    gate_part = gate_up_train.shape[2]
+    width = 2 * part
+    fine = row_width // n_col
+    bf16, f32 = jnp.bfloat16, jnp.float32
+    dma = pltpu.SemaphoreType.DMA
+    vmem, anywhere = pl.BlockSpec(memory_space=pltpu.VMEM), pl.BlockSpec(memory_space=pl.ANY)
+    q_piece = pltpu.VMEM((n_col, 3, fine, part), bf16)
+    g_piece = pltpu.VMEM((n_col, 2, fine, gate_part), bf16)
+    return pl.pallas_call(
+        functools.partial(sync_body, n_row=n_row, n_col=n_col),
+        out_shape=(
+            jax.ShapeDtypeStruct((3, tok, width), f32),
+            jax.ShapeDtypeStruct((3, n_row, fine, width), bf16),
+            jax.ShapeDtypeStruct((2, n_row, fine, 2 * gate_part), bf16),
+            jax.ShapeDtypeStruct((n_row * o_weight.shape[0], width_model // n_row), bf16),
+        ),
+        in_specs=[vmem, anywhere, vmem, anywhere],
+        out_specs=(vmem, vmem, vmem, anywhere),
+        scratch_shapes=[
+            pltpu.VMEM((n_col, tok, n_row * fine), bf16),
+            q_piece, q_piece, q_piece, q_piece,
+            pltpu.VMEM((n_col // 2, 2, 3, n_row * fine, width), bf16),
+            pltpu.VMEM((2, gate_part, row_width), f32),
+            g_piece, g_piece, g_piece, g_piece,
+            dma((3, n_col)),
+            dma((3, n_col)),
+            dma((3, n_col)),
+            dma((3, n_col)),
+            dma((n_col // 2, 2, 4)),
+            dma((n_col // 2, 2, 2)),
+            dma((n_row,)),
+            dma((n_row,)),
+            dma((n_row, 2)),
+            dma((3,)),
+        ],
+        compiler_params=pltpu.CompilerParams(
+            collective_id=1, has_side_effects=True, vmem_limit_bytes=60 << 20
+        ),
+        cost_estimate=pl.CostEstimate(
+            flops=2 * 3 * tok * width_model * width, bytes_accessed=30_000_000, transcendentals=0
+        ),
+        name="sync_weights",
+    )(qkv_train.swapaxes(1, 2), gate_up_train.swapaxes(1, 2), hidden, o_weight)
+
+
 def local(
     hidden, lengths, owner, page_table, qkv_train, qk_gain, o_weight, post_gain, gate_up_train
 ):
@@ -138,37 +543,14 @@
     model_width = hidden.shape[1]
     row_width = model_width // n_row
     col_block = row_width // n_col
-    trainer_qkv = qkv_train.astype(jnp.bfloat16)
-    trainer_gate_up = gate_up_train.astype(jnp.bfloat16)
-    server_qkv, server_gate_up = (
-        lax.all_to_all(
-            lax.all_to_all(trainer_qkv, "col", split_axis=1, concat_axis=2, tiled=True),
-            "row",
-            split_axis=2,
-            concat_axis=1,
-            tiled=True,
-        ),
-        lax.all_to_all(
-            lax.all_to_all(trainer_gate_up, "col", split_axis=1, concat_axis=2, tiled=True),
-            "row",
-            split_axis=2,
-            concat_axis=1,
-            tiled=True,
-        ),
-    )
-    heads_width = server_qkv.shape[2]
+    projected, weight_blocks, gate_up_blocks, o_columns = sync_weights(
+        qkv_train, gate_up_train, hidden, o_weight, n_row, n_col
+    )
+    heads_width = projected.shape[2]
     local_heads = heads_width // HD
-    weight_blocks = server_qkv.reshape(3, n_row, col_block, heads_width)
-    gate_up_blocks = server_gate_up.reshape(2, n_row, col_block, server_gate_up.shape[2])
-    hidden_three = hidden.reshape(tok_rows, n_row, row_width)
-    shard_piece = lax.all_gather(weight_blocks, "col", axis=2, tiled=True)
-    shards = shard_piece.shape[2] // col_block
-    projected = jnp.einsum(
-        "trb,jrbh->tjh", hidden_three, shard_piece, preferred_element_type=jnp.float32
-    )
-    query_rows = projected[:, 0]
-    key_rows = projected[:, 1]
-    value_rows = projected[:, 2]
+    query_rows = projected[0]
+    key_rows = projected[1]
+    value_rows = projected[2]
     query_squares, key_squares = lax.psum(
         (jnp.sum(query_rows * query_rows, axis=1), jnp.sum(key_rows * key_rows, axis=1)), "row"
     )
@@ -207,7 +589,6 @@
     first = jnp.stack([col_index * tok_rows, first_key]).astype(jnp.int32)
     attention = attend(first, token_start[:, None], query_rot, kv, span)
 
-    o_columns = lax.all_to_all(o_weight, "row", split_axis=1, concat_axis=0, tiled=True)
     attention_all = lax.all_gather(attention, "row", axis=1, tiled=True)
     own_out = jnp.dot(attention_all, o_columns, preferred_element_type=jnp.float32)
     out_squares = lax.psum(jnp.sum(own_out * own_out, axis=1), "row")

time: 467 us -> 320 us (0.69)
  Pallas kernels: 15.6 us -> 135 us
  waiting for transfers between devices: 216 us -> 109 us
  local copies, waits for them, and re-layouts: 99.1 us -> 8.74 us
  blocking collectives: 81.7 us -> 38.9 us
  starting transfers between devices: 13.7 us -> 0.26 us
  matrix products: 13.5 us -> 4.5 us
    pallas_call x0 -> x1, Pallas kernels: none -> 120 us  [sync_weights(): pl.pallas_call(functools.partial(sync_body, n_row=n_row, n_col=n_col), ou...]
    all_gather x1 -> x0, waiting for transfers between devices: 81.9 us -> none  [local(): shard_piece = lax.all_gather(weight_blocks, 'col', axis=2, tiled=True)]
    all_to_all x3 -> x0, waiting for transfers between devices: 57.5 us -> none  [the longest x1 29.3 us: local(): lax.all_to_all(lax.all_to_all(trainer_gate_up, 'col', split_axis=1, conca...]
    all_to_all x7 -> x0, local copies, waits for them, and re-layouts: 45.6 us -> none  [the longest x1 15.7 us: local(): lax.all_to_all(lax.all_to_all(trainer_gate_up, 'col', split_axis=1, conca...]
    all_to_all x2 -> x0, blocking collectives: 45.2 us -> none  [the longest x1 28.2 us: local(): lax.all_to_all(trainer_qkv, 'col', split_axis=1, concat_axis=2, tiled=True)]
    unnamed x19 -> x16, local copies, waits for them, and re-layouts: 46.1 us -> 6.7 us
    all_gather x1, waiting for transfers between devices: 0.01 us -> 36 us  [local(): attention_all = lax.all_gather(attention, 'row', axis=1, tiled=True)]
    all_to_all x3 -> x0, starting transfers between devices: 13.4 us -> none  [the longest x1 4.71 us: local(): lax.all_to_all(lax.all_to_all(trainer_gate_up, 'col', split_axis=1, conca...]
  transfers between devices with their start and end apart: 6 -> 2, of which waited for: 4 -> 2; matrix products, arithmetic and copies ran while one was open for 17% -> 1% of each run, Pallas kernels for 3% -> 2%
where the time goes in v2:
time: 320 us
  Pallas kernels  135 us (42%)
  waiting for transfers between devices  109 us (34%)
  blocking collectives  38.9 us (12%)
  between operations  14.2 us (4%)
  other arithmetic  9.06 us (3%)
  local copies, waits for them, and re-layouts  8.74 us (3%)
  matrix products  4.5 us (1%)
    pallas_call x1, Pallas kernels, sync_weights(): pl.pallas_call(functools.partial(sync_body, n_row=n_row, n_col=n_col), ou...  120 us
    all_gather x1, waiting for transfers between devices, local(): lax.all_gather(jnp.stack([key_rot, value_flat]), 'col', axis=1, tiled=True)  73 us
    all_gather x1, waiting for transfers between devices, local(): attention_all = lax.all_gather(attention, 'row', axis=1, tiled=True)  36 us
    psum x1, blocking collectives, local(): lax.psum((jnp.sum(query_rows * query_rows, axis=1), jnp.sum(key_rows * ke...  20.9 us
    psum x1, blocking collectives, local(): out_squares = lax.psum(jnp.sum(own_out * own_out, axis=1), 'row')  17.9 us
    pallas_call x1, Pallas kernels, attend(): pl.pallas_call(functools.partial(attend_body, span=span), out_shape=jax.S...  9.46 us
    unnamed x16, local copies, waits for them, and re-layouts  6.7 us
  transfers between devices with their start and end apart: 2, of which 2 were waited for; matrix products, arithmetic and copies ran while one was open for 1% of the time, Pallas kernels for 2%

profile of v2, /device:TPU:0, one launch (start us, length us, event | category | flops | bytes accessed | tf_op | source)
XLA Modules:
  0.0 319.8 jit_solution(8866875560306861807)
XLA Ops:
  7.2 119.7 %sync_weights.1 = (f32[3,320,384]{2,1,0:T(8,128)}, bf16[3,8,40,384]{3,2,1,0:T(8,128)(2,1)}, bf16[2,8,40,1728]{3,2,1,0:T(8,128)(2,1)}, bf16[3072,640]{1,0:T(8,128)(2,1)}) custom-call(f32[3,192,640]{2,1,0:T(8,128)} %bitcast.29, f32[2,864,640]{2,1,0:T(8,128)} %bitcast.28, bf16[320,5120]{1,0:T(8,128)(2,1)} %hid_ref.1, bf16[384,5120]{1,0:T(8,128)(2,1)} %ow_hbm.1), custom_call_target="tpu_custom_call" | custom-call | flops 3774873600 | bytes 30000000 | tf_op jit(solution)/shard_map/sync_weights/pallas_call | solution.py:498
  127.0 1.4 multiply_reduce_fusion.1
  128.4 1.1 slice.55
  129.4 0.2 copy.19
  129.7 0.2 reduce-window.8
  129.9 0.7 select_reduce_fusion.3
  130.7 0.1 select_reduce_fusion
  130.8 0.2 copy.18
  131.0 20.9 %all-reduce = (f32[320]{0:T(512)S(1)}, f32[320]{0:T(512)S(1)}) all-reduce(f32[320]{0:T(512)S(1)} %get-tuple-element.13, f32[320]{0:T(512)S(1)} %get-tuple-element.12), channel_id=1, replica_groups=mesh['row'=8,'col'=16] {'row'}, use_global_device_ids=true, to_apply=%region_4.0 | all-reduce | flops 640 | bytes 5120 | tf_op jit(solution)/shard_map/psum | solution.py:554
  152.0 0.4 multiply_cosine_fusion
  152.4 0.1 multiply_multiply_fusion
  152.5 0.1 multiply_multiply_fusion.1
  152.7 0.2 subtract_convert_fusion
  152.9 0.2 copy.20
  153.1 0.8 pad_maximum_fusion
  153.9 0.2 all-gather.5.cloned.1.call-start
  154.2 0.1 broadcast_in_dim.60.start_ref
  154.3 0.2 copy.22.query_ref
  154.6 73.0 %all-gather.3.cloned.1.call-done.kv_ref = bf16[2,5120,384]{2,1,0:T(8,128)(2,1)} async-done(((bf16[2,320,384]{2,1,0:T(8,128)(2,1)}), bf16[2,5120,384]{2,1,0:T(8,128)(2,1)}) %all-gather.3.cloned.1.call-update) | async-done | bytes 7864336 | tf_op jit(solution)/shard_map/all_gather | solution.py:572
  227.6 9.5 %attend.1 = bf16[320,384]{1,0:T(8,128)(2,1)} custom-call(s32[2]{0:T(128)S(1)} %pad_add_fusion.first_ref, s32[320,1]{1,0:T(8,128)S(1)} %broadcast_in_dim.60.start_ref, bf16[320,384]{1,0:T(8,128)(2,1)S(1)} %copy.22.query_ref, bf16[2,5120,384]{2,1,0:T(8,128)(2,1)} %all-gather.3.cloned.1.call-done.kv_ref), custom_call_target="tpu_custom_call" | custom-call | flops 1258291200 | bytes 8000000 | tf_op jit(solution)/shard_map/attend/pallas_call | solution.py:114
  237.1 0.6 reduce_or.9
  237.7 0.1 select_reduce_fusion.1
  237.8 0.6 broadcast_select_fusion
  238.4 1.4 pad_add_fusion.1.meta_ref
  239.8 3.2 %copy-done = bf16[2,5120,384]{2,1,0:T(8,128)(2,1)S(1)} copy-done((bf16[2,5120,384]{2,1,0:T(8,128)(2,1)S(1)}, bf16[2,5120,384]{2,1,0:T(8,128)(2,1)}, u32[]{:S(2)}) %copy-start) | copy-done | bytes 7864344
  243.1 6.1 %cache_pages.1 = bf16[16,2,128,384]{3,2,1,0:T(8,128)(2,1)} custom-call(s32[18]{0:T(128)S(1)} %pad_add_fusion.1.meta_ref, bf16[2,5120,384]{2,1,0:T(8,128)(2,1)S(1)} %copy-done), custom_call_target="tpu_custom_call" | custom-call | flops 10000000 | bytes 11000000 | tf_op jit(solution)/shard_map/cache_pages/pallas_call | solution.py:77
  249.2 36.0 %all-gather.5.cloned.1.call-done = bf16[320,3072]{1,0:T(8,128)(2,1)} async-done(((bf16[320,384]{1,0:T(8,128)(2,1)}), bf16[320,3072]{1,0:T(8,128)(2,1)}) %all-gather.5.cloned.1.call-update) | async-done | bytes 1966096 | tf_op jit(solution)/shard_map/all_gather | solution.py:592
  285.2 4.5 %multiply_reduce_fusion = (f32[320]{0:T(512)S(1)}, f32[320,640]{1,0:T(8,128)S(1)}) fusion(bf16[320,3072]{1,0:T(8,128)(2,1)} %all-gather.5.cloned.1.call-done, bf16[3072,640]{1,0:T(8,128)(2,1)} %get-tuple-element.9), kind=kOutput, calls=%fused_computation.1 | convolution fusion | flops 1258700544 | bytes 6718720 | tf_op jit(solution)/shard_map/dot_general | solution.py:593
  289.7 17.9 %psum.23 = f32[320]{0:T(512)S(1)} all-reduce(f32[320]{0:T(512)S(1)} %get-tuple-element.32), channel_id=1, replica_groups=mesh['row'=8,'col'=16] {'row'}, use_global_device_ids=true, to_apply=%region_8.9 | all-reduce | flops 320 | bytes 2560 | tf_op jit(solution)/shard_map/psum | solution.py:594
  307.6 2.0 add_convert_fusion
  309.6 2.1 copy.25
  311.6 1.4 copy.26
  (26 shorter events, 0.4 us)
Async XLA Ops:
  7.2 220.4 %all-gather.3.cloned.1.call-start = ((), (), s32[]{:S(2)}) async-start(), calls=%async_computation | async-start | bytes 8355840 | tf_op jit(solution)/shard_map/all_gather | solution.py:572
  126.9 2.8 copy-start.3
  126.9 2.8 copy-start.5
  126.9 3.0 copy-start.6
  153.9 131.2 %all-gather.5.cloned.1.call-start = ((), (), s32[]{:S(2)}) async-start(), calls=%async_computation.1 | async-start | bytes 2211840 | tf_op jit(solution)/shard_map/all_gather | solution.py:592
  154.6 83.1 %copy-start.4 = (s32[4,16]{1,0:T(4,128)S(1)}, s32[4,16]{1,0:T(4,128)}, u32[]{:S(2)}) copy-start(s32[4,16]{1,0:T(4,128)} %param.12) | copy-start | bytes 772
  239.8 3.2 %copy-start = (bf16[2,5120,384]{2,1,0:T(8,128)(2,1)S(1)}, bf16[2,5120,384]{2,1,0:T(8,128)(2,1)}, u32[]{:S(2)}) copy-start(bf16[2,5120,384]{2,1,0:T(8,128)(2,1)} %all-gather.3.cloned.1.call-done.kv_ref) | copy-start | bytes 23592964
  285.2 22.4 %copy-start.2 = (f32[640]{0:T(1024)S(1)}, f32[640]{0:T(1024)}, u32[]{:S(2)}) copy-start(f32[640]{0:T(1024)} %param.16) | copy-start | bytes 7684
  289.7 21.9 %copy-start.1 = (bf16[2,8,40,1728]{3,2,1,0:T(8,128)(2,1)S(1)}, bf16[2,8,40,1728]{3,2,1,0:T(8,128)(2,1)}, u32[]{:S(2)}) copy-start(bf16[2,8,40,1728]{3,2,1,0:T(8,128)(2,1)} %get-tuple-element.43) | copy-start | bytes 6635524
Sparse Core Ops, SparseCore 0:
  154.1 73.4 all-gather.2
  237.2 47.9 all-gather.4

commit v3 on v2

--- a/solution.py
+++ b/solution.py
@@ -17,27 +17,6 @@
 norm_epsilon = 1e-06
 rope_theta = 500000.0
 big_negative = -1e30
-
-
-def inverse_rms(squares, features):
-    return lax.rsqrt(squares / features + norm_epsilon)
-
-
-def rotate_heads(inputs, positions):
-    half_dim = inputs.shape[-1] // 2
-    frequency = rope_theta ** (-2.0 * jnp.arange(half_dim, dtype=jnp.float32) / inputs.shape[-1])
-    angles = positions.astype(jnp.float32)[:, None] * frequency[None, :]
-    cosine = jnp.cos(angles)[:, None, :]
-    sine_part = jnp.sin(angles)[:, None, :]
-    lower_half = inputs[..., :half_dim]
-    upper_half = inputs[..., half_dim:]
-    return jnp.concatenate(
-        [
-            lower_half * cosine - upper_half * sine_part,
-            upper_half * cosine + lower_half * sine_part,
-        ],
-        axis=-1,
-    )
 
 
 def locate_tokens(token_index, lengths):
@@ -51,80 +30,6 @@
 
 ALIGN = 16
 WINDOW = PAGE + ALIGN
-
-
-def cache_body(meta_ref, kv_ref, out_ref):
-    tokens = kv_ref.shape[1]
-    start, length = meta_ref[0], meta_ref[1]
-
-    @pl.loop(0, PAGES)
-    def _(page):
-        first = jnp.minimum(start + page * PAGE, tokens - 1)
-        base = jnp.minimum((first // ALIGN) * ALIGN, tokens - WINDOW)
-        base = pl.multiple_of(base, ALIGN)
-        shift = first - base
-        slot = meta_ref[2 + page]
-        rows = lax.broadcasted_iota(jnp.int32, (PAGE, 1), 0) + page * PAGE
-        inside = rows < length
-        for part in range(2):
-            piece = kv_ref[part, pl.ds(base, WINDOW), :].astype(jnp.float32)
-            piece = pltpu.roll(piece, lax.rem(WINDOW - shift, WINDOW), 0)[:PAGE]
-            out_ref[slot, part] = jnp.where(inside, piece, 0.0).astype(jnp.bfloat16)
-
-
-def build_cache(meta, kv):
-    width = kv.shape[2]
-    return pl.pallas_call(
-        cache_body,
-        out_shape=jax.ShapeDtypeStruct((PAGES, 2, PAGE, width), jnp.bfloat16),
-        in_specs=[
-            pl.BlockSpec(memory_space=pltpu.SMEM),
-            pl.BlockSpec(memory_space=pltpu.VMEM),
-        ],
-        out_specs=pl.BlockSpec(memory_space=pltpu.VMEM),
-        compiler_params=pltpu.CompilerParams(vmem_limit_bytes=40 << 20),
-        cost_estimate=pl.CostEstimate(flops=10_000_000, bytes_accessed=11_000_000, transcendentals=0),
-        name="cache_pages",
-    )(meta, kv)
-
-
-def attend_body(first_ref, start_ref, query_ref, kv_ref, out_ref, *, span):
-    rows = query_ref.shape[0]
-    heads = query_ref.shape[1] // HD
-    first_query, first_key = first_ref[0], first_ref[1]
-    first_key = pl.multiple_of(first_key, 64)
-    query_index = first_query + lax.broadcasted_iota(jnp.int32, (rows, 1), 0)
-    key_index = first_key + lax.broadcasted_iota(jnp.int32, (1, span), 1)
-    allowed = (key_index <= query_index) & (key_index >= start_ref[...])
-    for head in range(heads):
-        lanes = slice(head * HD, (head + 1) * HD)
-        keys = kv_ref[0, pl.ds(first_key, span), lanes]
-        values = kv_ref[1, pl.ds(first_key, span), lanes]
-        scores = lax.dot_general(
-            query_ref[:, lanes], keys, (((1,), (1,)), ((), ())), preferred_element_type=jnp.float32
-        ) * (1.0 / math.sqrt(HD))
-        scores = jnp.where(allowed, scores, big_negative)
-        exponent = jnp.exp(scores - jnp.max(scores, axis=1, keepdims=True))
-        total = jnp.sum(exponent, axis=1, keepdims=True)
-        mixed = jnp.dot(exponent.astype(jnp.bfloat16), values, preferred_element_type=jnp.float32)
-        out_ref[:, lanes] = (mixed / total).astype(jnp.bfloat16)
-
-
-def attend(first, start, query, kv, span):
-    return pl.pallas_call(
-        functools.partial(attend_body, span=span),
-        out_shape=jax.ShapeDtypeStruct(query.shape, jnp.bfloat16),
-        in_specs=[pl.BlockSpec(memory_space=pltpu.SMEM)]
-        + [pl.BlockSpec(memory_space=pltpu.VMEM)] * 3,
-        out_specs=pl.BlockSpec(memory_space=pltpu.VMEM),
-        compiler_params=pltpu.CompilerParams(vmem_limit_bytes=48 << 20),
-        cost_estimate=pl.CostEstimate(
-            flops=4 * query.shape[0] * span * query.shape[1],
-            bytes_accessed=8_000_000,
-            transcendentals=3 * query.shape[0] * span,
-        ),
-        name="attend",
-    )(first, start, query, kv)
 
 
 def rdma(src, dst, send_sem, recv_sem, device):
@@ -255,76 +160,95 @@
         each(16, each_piece)
 
 
-class ColGather:
-    def __init__(self, me, view, send, recv):
-        self.me, self.view, self.send, self.recv = me, view, send, recv
+class Gather:
+    def __init__(self, me, over_col, view, send, recv):
+        self.me, self.over_col, self.view, self.send, self.recv = me, over_col, view, send, recv
+        self.hand = (3,) if over_col else ()
         self.sent = []
 
-    def chip(self, dz, dx):
-        return wrap(self.me.zh + dz, 2) * 4 + wrap(self.me.x + dx, 4)
-
-    def copy(self, chip, half, kind):
+    def block(self, dz, dr):
         me = self.me
-        device = [
-            me.at(x=wrap(me.x + 1, 4)), me.at(x=wrap(me.x - 1, 4)), me.at(zh=1 - me.zh),
-            me.at(core=1 - me.core),
-        ][kind]
-        ref = self.view(chip, me.core, half)
+        if self.over_col:
+            return wrap(me.zh + dz, 2) * 4 + wrap(me.x + dr, 4)
+        return wrap(me.y + dr, 4) * 2 + wrap(me.zl + dz, 2)
+
+    def copy(self, dz, dr, half, kind):
+        me = self.me
+        if kind == 3:
+            device = me.at(core=1 - me.core)
+        elif kind == 2:
+            device = me.at(zh=1 - me.zh) if self.over_col else me.at(zl=1 - me.zl)
+        else:
+            turn = 1 - 2 * kind
+            device = (
+                me.at(x=wrap(me.x + turn, 4)) if self.over_col else me.at(y=wrap(me.y + turn, 4))
+            )
+        block = self.block(dz, dr)
+        ref = self.view(block, me.core, half)
         return rdma(
-            ref, ref, self.send.at[chip, half, kind], self.recv.at[chip, me.core, half], device
-        )
-
-    def go(self, chip, half, *kinds):
-        for kind in kinds:
-            self.copy(chip, half, kind).start()
-            self.sent.append((chip, half, kind))
-
-    def got(self, chip, core, half):
+            ref, ref, self.send.at[block, half, kind], self.recv.at[block, me.core, half], device
+        )
+
+    def go(self, dz, dr, half, *kinds):
+        for kind in kinds + self.hand:
+            self.copy(dz, dr, half, kind).start()
+            self.sent.append((dz, dr, half, kind))
+
+    def got(self, dz, dr, half, sibling=False):
+        block = self.block(dz, dr)
+        core = 1 - self.me.core if sibling else self.me.core
         arrived(
-            self.view(chip, core, half), self.recv.at[chip, core, half], self.send.at[0, 0, 0],
+            self.view(block, core, half), self.recv.at[block, core, half], self.send.at[0, 0, 0],
             self.me.here,
         )
 
-    def start(self):
-        for half in range(2):
-            self.go(self.chip(0, 0), half, 2, 0, 1, 3)
+    def start(self, half):
+        self.go(0, 0, half, 2, 0, 1)
 
     def z_turn(self):
         for half in range(2):
-            self.got(self.chip(1, 0), self.me.core, half)
-            self.go(self.chip(1, 0), half, 0, 1, 3)
+            self.got(1, 0, half)
+            self.go(1, 0, half, 0, 1)
 
     def x_turn(self, dz, *more):
-        left, right = self.chip(dz, -1), self.chip(dz, 1)
-        core = self.me.core
-        self.got(left, core, 0)
-        self.go(left, 0, 0, *more, 3)
-        self.got(right, core, 1)
-        self.go(right, 1, 1, *more, 3)
-        self.got(left, core, 1)
-        self.go(left, 1, *more, 3)
-        self.got(right, core, 0)
-        self.go(right, 0, *more, 3)
+        self.got(dz, -1, 0)
+        self.go(dz, -1, 0, 0, *more)
+        self.got(dz, 1, 0)
+        self.go(dz, 1, 0, *more)
+        self.got(dz, 1, 1)
+        self.go(dz, 1, 1, 1, *more)
+        self.got(dz, -1, 1)
+        self.go(dz, -1, 1, *more)
 
     def x_end(self, dz, *more):
         for half in range(2):
-            self.got(self.chip(dz, 2), self.me.core, half)
-            self.go(self.chip(dz, 2), half, *more, 3)
+            self.got(dz, 2, half)
+            self.go(dz, 2, half, *more)
 
     def z_end(self):
-        for dx in (0, -1, 1, 2):
-            for half in range(2):
-                self.got(self.chip(1, dx), self.me.core, half)
-                self.go(self.chip(1, dx), half, 3)
-
-    def sibling(self, dz, dx):
         for half in range(2):
-            self.got(self.chip(dz, dx), 1 - self.me.core, half)
+            for dr in (0, -1, 1, 2):
+                self.got(1, dr, half)
+                self.go(1, dr, half)
+
+    def sibling(self, dz, dr):
+        for half in range(2):
+            self.got(dz, dr, half, sibling=True)
 
     def drain(self):
         for which in self.sent:
             self.copy(*which).wait_send()
         self.sent = []
+
+
+def by_core(me, run):
+    @pl.when(me.core == 0)
+    def _():
+        run(True)
+
+    @pl.when(me.core == 1)
+    def _():
+        run(False)
 
 
 def sync_body(
@@ -387,8 +311,9 @@
             w_all[me.chip, core, j, pair * 2 * fine:(pair + 1) * 2 * fine, :] = both
 
     depth = w_all.shape[3] // 2
-    weights = ColGather(me, lambda p, k, h: w_all.at[p, k, :, h * depth:(h + 1) * depth, :], w_send, w_recv)
-    weights.start()
+    weights = Gather(me, True, lambda p, k, h: w_all.at[p, k, :, h * depth:(h + 1) * depth, :], w_send, w_recv)
+    weights.start(0)
+    weights.start(1)
 
     own_rows = ow_hbm.shape[0]
     half_o = own_rows // 2
@@ -532,71 +457,314 @@
     )(qkv_train.swapaxes(1, 2), gate_up_train.swapaxes(1, 2), hidden, o_weight)
 
 
+def column_of(sums, at_row):
+    pick = (lax.broadcasted_iota(jnp.int32, (8, 128), 0) == at_row).astype(jnp.float32)
+    return lax.dot_general(
+        sums, pick, (((0,), (0,)), ((), ())),
+        precision=lax.Precision.HIGHEST, preferred_element_type=jnp.float32,
+    )
+
+
+def lane_sums(values):
+    return lax.dot_general(
+        jnp.ones((8, values.shape[1]), jnp.float32), values * values, (((1,), (1,)), ((), ())),
+        precision=lax.Precision.HIGHEST, preferred_element_type=jnp.float32,
+    )
+
+
+def layer_body(
+    proj_ref, cos_ref, sin_ref, gain_ref, start_ref, ocol_ref, post_ref, hid_hbm,
+    out_ref, kv_out,
+    query, kv, mixed_all, residual, sq_in, sq_out,
+    kv_send, kv_recv, a_send, a_recv, s_send, s_recv, t_send, t_recv, local_sem,
+    *, n_row, n_col,
+):
+    me = Place()
+    row, col = me.row, me.col
+    bf16, f32 = jnp.bfloat16, jnp.float32
+    tok, width = query.shape
+    heads = width // HD
+    out_width = out_ref.shape[1]
+    keep = pltpu.make_async_copy(
+        hid_hbm.at[:, pl.ds(pl.multiple_of(row * out_width, 128), out_width)], residual, local_sem.at[0]
+    )
+    keep.start()
+
+    barrier = pltpu.get_barrier_semaphore()
+    signal(barrier, me.at(x=wrap(me.x + 1, 4)))
+    signal(barrier, me.at(x=wrap(me.x - 1, 4)))
+    signal(barrier, me.at(zh=1 - me.zh))
+    signal(barrier, me.at(core=1 - me.core))
+    for i in range(1, n_row):
+        signal(barrier, (lax.rem(row + i, n_row), col))
+
+    own = pl.ds(pl.multiple_of(col * tok, 64), tok)
+    kv[1, own, :] = proj_ref[2].astype(bf16)
+    top = lax.broadcasted_iota(jnp.int32, (8, tok), 0) < 4
+    sq_in[row] = jnp.where(top, lane_sums(proj_ref[0]), lane_sums(proj_ref[1]))
+    pl.semaphore_wait(barrier, 4 + n_row - 1)
+
+    def share(buffer, send, recv, i):
+        return rdma(
+            buffer.at[row], buffer.at[row], send.at[i], recv.at[row],
+            (lax.rem(row + 1 + i, n_row), col),
+        )
+
+    def shared(buffer, send, recv):
+        def wait(i):
+            src = lax.rem(row + 1 + i, n_row)
+            arrived(buffer.at[src], recv.at[src], send.at[0], me.here)
+
+        each(n_row - 1, wait)
+        total = buffer[0]
+        for src in range(1, n_row):
+            total = total + buffer[src]
+        return total
+
+    each(n_row - 1, lambda i: share(sq_in, s_send, s_recv, i).start())
+
+    def tokens_of(block, core, half):
+        rows = pl.ds(pl.multiple_of((2 * block + core) * tok, 64), tok)
+        return kv.at[1 - half, rows, :]
+
+    gathers = [Gather(me, True, tokens_of, kv_send, kv_recv) for _ in range(2)]
+    first_sends = Gather(me, True, tokens_of, kv_send, kv_recv)
+    first_sends.start(0)
+
+    squares = shared(sq_in, s_send, s_recv)
+    cosine, sine = cos_ref[...], sin_ref[...]
+    for which in (1, 0):
+        scale = lax.rsqrt(column_of(squares, 4 * which) / (n_row * width) + norm_epsilon)
+        for head in range(heads):
+            lanes = slice(head * HD, (head + 1) * HD)
+            x = proj_ref[which, :, lanes] * scale * gain_ref[which:which + 1, lanes]
+            turned = (x * cosine + pltpu.roll(x, HD // 2, 1) * sine).astype(bf16)
+            if which == 1:
+                kv[0, own, lanes] = turned
+            else:
+                query[:, lanes] = turned
+        if which == 1:
+            first_sends.start(1)
+
+    def kv_gather(z_first):
+        g = gathers[0 if z_first else 1]
+        if z_first:
+            g.z_turn()
+            g.x_turn(0)
+            g.x_turn(1)
+            g.x_end(0)
+            g.x_end(1)
+        else:
+            g.x_turn(0, 2)
+            g.x_end(0, 2)
+            g.z_end()
+
+    by_core(me, kv_gather)
+    for dz in range(2):
+        for dx in range(4):
+            if (dz, dx) != (0, 0):
+                gathers[0].sibling(dz, dx)
+    gathers[0].sibling(0, 0)
+
+    give = pltpu.make_async_copy(kv, kv_out, local_sem.at[1])
+    give.start()
+
+    reach = -(-(LMAX - 1) // tok)
+    span = min(reach + 1, n_col) * tok
+    first_key = pl.multiple_of(jnp.maximum(col - reach, 0) * tok, 64)
+    query_index = col * tok + lax.broadcasted_iota(jnp.int32, (tok, 1), 0)
+    key_index = first_key + lax.broadcasted_iota(jnp.int32, (1, span), 1)
+    allowed = (key_index <= query_index) & (key_index >= start_ref[...])
+    for head in range(heads):
+        lanes = slice(head * HD, (head + 1) * HD)
+        keys = kv[0, pl.ds(first_key, span), lanes]
+        values = kv[1, pl.ds(first_key, span), lanes]
+        scores = lax.dot_general(
+            query[:, lanes], keys, (((1,), (1,)), ((), ())), preferred_element_type=f32
+        ) * (1.0 / math.sqrt(HD))
+        scores = jnp.where(allowed, scores, big_negative)
+        exponent = jnp.exp(scores - jnp.max(scores, axis=1, keepdims=True))
+        total = jnp.sum(exponent, axis=1, keepdims=True)
+        mixed = jnp.dot(exponent.astype(bf16), values, preferred_element_type=f32)
+        mixed_all[row, :, lanes] = (mixed / total).astype(bf16)
+
+    half_tok = tok // 2
+    row_gathers = [
+        Gather(
+            me, False,
+            lambda block, core, half: mixed_all.at[block, pl.ds(half * half_tok, half_tok), :],
+            a_send, a_recv,
+        )
+        for _ in range(2)
+    ]
+
+    def row_gather(z_first):
+        g = row_gathers[0 if z_first else 1]
+        g.start(0)
+        g.start(1)
+        if z_first:
+            g.z_turn()
+            g.x_turn(0)
+            g.x_turn(1)
+            g.x_end(0)
+            g.x_end(1)
+        else:
+            g.x_turn(0, 2)
+            g.x_end(0, 2)
+            g.z_end()
+
+    by_core(me, row_gather)
+
+    product = jnp.zeros((tok, out_width), f32)
+    for src in range(n_row):
+        product += jnp.dot(
+            mixed_all[src], ocol_ref[src * width:(src + 1) * width, :], preferred_element_type=f32
+        )
+    sq_out[row] = lane_sums(product)
+    each(n_row - 1, lambda i: share(sq_out, t_send, t_recv, i).start())
+    keep.wait()
+
+    each(n_row - 1, lambda i: share(sq_in, s_send, s_recv, i).wait_send())
+    first_sends.drain()
+
+    def drain(z_first):
+        which = 0 if z_first else 1
+        gathers[which].drain()
+        row_gathers[which].drain()
+
+    by_core(me, drain)
+
+    scale = lax.rsqrt(column_of(shared(sq_out, t_send, t_recv), 0) / (n_row * out_width) + norm_epsilon)
+    for at in range(0, out_width, 128):
+        lanes = slice(at, at + 128)
+        out_ref[:, lanes] = (
+            residual[:, lanes].astype(f32) + product[:, lanes] * scale * post_ref[:, lanes]
+        ).astype(bf16)
+    each(n_row - 1, lambda i: share(sq_out, t_send, t_recv, i).wait_send())
+    give.wait()
+
+
+def attention_layer(projected, cosine, sine, gain, start, o_columns, post, hidden, n_row, n_col):
+    _, tok, width = projected.shape
+    out_width = o_columns.shape[1]
+    bf16, f32 = jnp.bfloat16, jnp.float32
+    dma = pltpu.SemaphoreType.DMA
+    vmem, anywhere = pl.BlockSpec(memory_space=pltpu.VMEM), pl.BlockSpec(memory_space=pl.ANY)
+    return pl.pallas_call(
+        functools.partial(layer_body, n_row=n_row, n_col=n_col),
+        out_shape=(
+            jax.ShapeDtypeStruct((tok, out_width), bf16),
+            jax.ShapeDtypeStruct((2, n_col * tok, width), bf16),
+        ),
+        in_specs=[vmem] * 7 + [anywhere],
+        out_specs=(vmem, anywhere),
+        scratch_shapes=[
+            pltpu.VMEM((tok, width), bf16),
+            pltpu.VMEM((2, n_col * tok, width), bf16),
+            pltpu.VMEM((n_row, tok, width), bf16),
+            pltpu.VMEM((tok, out_width), bf16),
+            pltpu.VMEM((n_row, 8, tok), f32),
+            pltpu.VMEM((n_row, 8, tok), f32),
+            dma((n_col // 2, 2, 4)),
+            dma((n_col // 2, 2, 2)),
+            dma((n_row, 2, 4)),
+            dma((n_row, 2, 2)),
+            dma((n_row,)),
+            dma((n_row,)),
+            dma((n_row,)),
+            dma((n_row,)),
+            dma((2,)),
+        ],
+        compiler_params=pltpu.CompilerParams(
+            collective_id=2, has_side_effects=True, vmem_limit_bytes=60 << 20
+        ),
+        cost_estimate=pl.CostEstimate(
+            flops=8_000_000_000, bytes_accessed=20_000_000, transcendentals=3_000_000
+        ),
+        name="attention_layer",
+    )(projected, cosine, sine, gain, start, o_columns, post, hidden)
+
+
+def cache_body(meta_ref, kv_hbm, out_ref, windows, sems):
+    tokens = kv_hbm.shape[1]
+    begin, length = meta_ref[0], meta_ref[1]
+
+    def locate(slot):
+        first = jnp.minimum(begin + meta_ref[2 + slot] * PAGE, tokens - 1)
+        base = pl.multiple_of(jnp.minimum((first // ALIGN) * ALIGN, tokens - WINDOW), ALIGN)
+        return first, base
+
+    def fetch(slot):
+        _, base = locate(slot)
+        return pltpu.make_async_copy(
+            kv_hbm.at[:, pl.ds(base, WINDOW), :], windows.at[slot], sems.at[slot]
+        )
+
+    each(PAGES, lambda slot: fetch(slot).start())
+
+    def place(slot):
+        fetch(slot).wait()
+        first, base = locate(slot)
+        turn = lax.rem(WINDOW - (first - base), WINDOW)
+        rows = lax.broadcasted_iota(jnp.int32, (PAGE, 1), 0) + meta_ref[2 + slot] * PAGE
+        for part in range(2):
+            piece = pltpu.roll(windows[slot, part].astype(jnp.float32), turn, 0)[:PAGE]
+            out_ref[slot, part] = jnp.where(rows < length, piece, 0.0).astype(jnp.bfloat16)
+
+    each(PAGES, place)
+
+
+def build_cache(meta, kv):
+    width = kv.shape[2]
+    return pl.pallas_call(
+        cache_body,
+        out_shape=jax.ShapeDtypeStruct((PAGES, 2, PAGE, width), jnp.bfloat16),
+        in_specs=[pl.BlockSpec(memory_space=pltpu.SMEM), pl.BlockSpec(memory_space=pl.ANY)],
+        out_specs=pl.BlockSpec(memory_space=pltpu.VMEM),
+        scratch_shapes=[
+            pltpu.VMEM((PAGES, 2, WINDOW, width), jnp.bfloat16),
+            pltpu.SemaphoreType.DMA((PAGES,)),
+        ],
+        compiler_params=pltpu.CompilerParams(vmem_limit_bytes=16 << 20),
+        cost_estimate=pl.CostEstimate(flops=10_000_000, bytes_accessed=7_000_000, transcendentals=0),
+        name="cache_pages",
+    )(meta, kv)
+
+
 def local(
     hidden, lengths, owner, page_table, qkv_train, qk_gain, o_weight, post_gain, gate_up_train
 ):
     n_row = lax.axis_size("row")
     n_col = lax.axis_size("col")
     col_index = lax.axis_index("col")
-    row_index = lax.axis_index("row")
     tok_rows = hidden.shape[0]
-    model_width = hidden.shape[1]
-    row_width = model_width // n_row
-    col_block = row_width // n_col
     projected, weight_blocks, gate_up_blocks, o_columns = sync_weights(
         qkv_train, gate_up_train, hidden, o_weight, n_row, n_col
     )
-    heads_width = projected.shape[2]
-    local_heads = heads_width // HD
-    query_rows = projected[0]
-    key_rows = projected[1]
-    value_rows = projected[2]
-    query_squares, key_squares = lax.psum(
-        (jnp.sum(query_rows * query_rows, axis=1), jnp.sum(key_rows * key_rows, axis=1)), "row"
-    )
-    full_heads = HEADS * HD
-    query_norm = query_rows * inverse_rms(query_squares, full_heads)[:, None] * qk_gain[0]
-    key_norm = key_rows * inverse_rms(key_squares, full_heads)[:, None] * qk_gain[1]
     token_index = col_index * tok_rows + jnp.arange(tok_rows, dtype=jnp.int32)
     token_start = locate_tokens(token_index, lengths)
-    position = token_index - token_start
-    query_rot = rotate_heads(query_norm.reshape(tok_rows, local_heads, HD), position).astype(
-        jnp.bfloat16
-    ).reshape(tok_rows, heads_width)
-    key_rot = (
-        rotate_heads(key_norm.reshape(tok_rows, local_heads, HD), position)
-        .astype(jnp.bfloat16)
-        .reshape(tok_rows, heads_width)
-    )
-    value_flat = value_rows.astype(jnp.bfloat16)
-    kv = lax.all_gather(jnp.stack([key_rot, value_flat]), "col", axis=1, tiled=True)
+    half_dim = HD // 2
+    frequency = rope_theta ** (-2.0 * jnp.arange(half_dim, dtype=jnp.float32) / HD)
+    angles = (token_index - token_start).astype(jnp.float32)[:, None] * frequency[None, :]
+    cosine, sine = jnp.cos(angles), jnp.sin(angles)
+    cosine = jnp.concatenate([cosine, cosine], axis=1)
+    sine = jnp.concatenate([-sine, sine], axis=1)
 
     prompt_starts = jnp.cumsum(lengths) - lengths
     owned = owner == col_index
     my_start = jnp.sum(jnp.where(owned, prompt_starts, 0))
     my_length = jnp.sum(jnp.where(owned, lengths, 0))
-    my_pages = jnp.where(
-        jnp.any(owned),
-        jnp.sum(jnp.where(owned[:, None], page_table, 0), axis=0),
-        jnp.arange(PAGES, dtype=jnp.int32),
-    )
-    meta = jnp.concatenate([jnp.stack([my_start, my_length]), my_pages]).astype(jnp.int32)
+    my_pages = jnp.sum(jnp.where(owned[:, None], page_table, 0), axis=0)
+    slots = jnp.arange(PAGES, dtype=jnp.int32)
+    page_of = jnp.sum(jnp.where(my_pages[None, :] == slots[:, None], slots[None, :], 0), axis=1)
+    page_of = jnp.where(my_length > 0, page_of, slots)
+    meta = jnp.concatenate([jnp.stack([my_start, my_length]), page_of]).astype(jnp.int32)
+
+    layer_out, kv = attention_layer(
+        projected, cosine, sine, qk_gain, token_start[:, None], o_columns,
+        post_gain[None, :], hidden, n_row, n_col,
+    )
     cache_pages = build_cache(meta, kv)
-
-    reach = -(-(LMAX - 1) // tok_rows)
-    span = min(reach + 1, n_col) * tok_rows
-    first_key = jnp.maximum(col_index - reach, 0) * tok_rows
-    first = jnp.stack([col_index * tok_rows, first_key]).astype(jnp.int32)
-    attention = attend(first, token_start[:, None], query_rot, kv, span)
-
-    attention_all = lax.all_gather(attention, "row", axis=1, tiled=True)
-    own_out = jnp.dot(attention_all, o_columns, preferred_element_type=jnp.float32)
-    out_squares = lax.psum(jnp.sum(own_out * own_out, axis=1), "row")
-    normalized = own_out * inverse_rms(out_squares, model_width)[:, None] * post_gain
-    residual = lax.dynamic_slice_in_dim(hidden, row_index * row_width, row_width, 1).astype(
-        jnp.float32
-    )
-    layer_out = (residual + normalized).astype(jnp.bfloat16)
     return (layer_out, cache_pages[None], weight_blocks, gate_up_blocks)
 
 

time: 320 us -> 223 us (0.70)
  waiting for transfers between devices: 109 us -> 0 us
  Pallas kernels: 135 us -> 206 us
  blocking collectives: 38.9 us -> 0 us
  between operations: 14.2 us -> 1.36 us
  matrix products: 4.5 us -> 0 us
    all_gather x2 -> x0, waiting for transfers between devices: 109 us -> none  [the longest x1 73 us: local(): lax.all_gather(jnp.stack([key_rot, value_flat]), 'col', axis=1, tiled=True)]
    pallas_call x1, Pallas kernels: 9.46 us -> 77.8 us  [attention_layer(): pl.pallas_call(functools.partial(layer_body, n_row=n_row, n_col=n_col), o...]
    psum x2 -> x0, blocking collectives: 38.9 us -> none  [the longest x1 20.9 us: local(): lax.psum((jnp.sum(query_rows * query_rows, axis=1), jnp.sum(key_rows * ke...]
    dot_general x1 -> x0, matrix products: 4.5 us -> none  [local(): jnp.dot(attention_all, o_columns, preferred_element_type=jnp.float32)]
    unnamed x16 -> x11, local copies, waits for them, and re-layouts: 6.7 us -> 6.51 us
  transfers between devices with their start and end apart: 2 -> 0, of which waited for: 2 -> 0; matrix products, arithmetic and copies ran while one was open for 1% -> 0% of each run, Pallas kernels for 2% -> 0%
where the time goes in v3:
time: 223 us; the launch traced here: 222 us
  Pallas kernels  206 us (92%)
  local copies, waits for them, and re-layouts  8.55 us (4%)
  other arithmetic  6.13 us (3%)
    pallas_call x1, Pallas kernels, sync_weights(): pl.pallas_call(functools.partial(sync_body, n_row=n_row, n_col=n_col), ou...  120 us
    pallas_call x1, Pallas kernels, attention_layer(): pl.pallas_call(functools.partial(layer_body, n_row=n_row, n_col=n_col), o...  77.8 us
    pallas_call x1, Pallas kernels, build_cache(): pl.pallas_call(cache_body, out_shape=jax.ShapeDtypeStruct((PAGES, 2, PAGE...  8.78 us
    unnamed x11, local copies, waits for them, and re-layouts  6.51 us

profile of v3, /device:TPU:0, one launch (start us, length us, event | category | flops | bytes accessed | tf_op | source)
XLA Modules:
  0.0 222.1 jit_solution(10375724026294152731)
XLA Ops:
  0.6 0.8 reduce-window.8
  1.5 1.3 select_reduce_fusion.4
  3.4 0.8 select_reduce_fusion.2
  4.2 0.1 select_reduce_fusion
  4.3 1.4 pad_add_fusion.meta_ref
  5.7 0.1 convert_reduce_fusion
  5.8 0.1 select_reduce_fusion.1
  5.9 1.3 broadcast_in_dim.61.post_ref
  7.2 0.8 reduce_sum.63.start_ref
  7.9 0.6 fusion
  8.6 0.9 pad_maximum_fusion
  9.5 119.5 %sync_weights.1 = (f32[3,320,384]{2,1,0:T(8,128)}, bf16[3,8,40,384]{3,2,1,0:T(8,128)(2,1)}, bf16[2,8,40,1728]{3,2,1,0:T(8,128)(2,1)}, bf16[3072,640]{1,0:T(8,128)(2,1)}) custom-call(f32[3,192,640]{2,1,0:T(8,128)} %bitcast.13, f32[2,864,640]{2,1,0:T(8,128)} %bitcast.12, bf16[320,5120]{1,0:T(8,128)(2,1)} %hid_hbm.1, bf16[384,5120]{1,0:T(8,128)(2,1)} %ow_hbm.1), custom_call_target="tpu_custom_call" | custom-call | flops 3774873600 | bytes 30000000 | tf_op jit(solution)/shard_map/sync_weights/pallas_call | solution.py:423
  129.0 77.8 %attention_layer.1 = (bf16[320,640]{1,0:T(8,128)(2,1)}, bf16[2,5120,384]{2,1,0:T(8,128)(2,1)}) custom-call(f32[3,320,384]{2,1,0:T(8,128)} %get-tuple-element.10.proj_ref, f32[320,128]{1,0:T(8,128)} %get-tuple-element.23.cos_ref, f32[320,128]{1,0:T(8,128)} %get-tuple-element.24.sin_ref, f32[2,384]{1,0:T(2,128)} %gain_ref.1, s32[320,1]{1,0:T(8,128)} %reduce_sum.63.start_ref, ...), custom_call_target="tpu_custom_call" | custom-call | flops 8000000000 | bytes 20000000 | tf_op jit(solution)/shard_map/attention_layer/pallas_call | solution.py:653
  206.8 0.0 copy-start
  206.8 3.2 %copy-done = bf16[2,5120,384]{2,1,0:T(8,128)(2,1)S(1)} copy-done((bf16[2,5120,384]{2,1,0:T(8,128)(2,1)S(1)}, bf16[2,5120,384]{2,1,0:T(8,128)(2,1)}, u32[]{:S(2)}) %copy-start) | copy-done | bytes 7864344
  210.0 0.0 copy-start.3
  210.1 0.0 copy-start.2
  210.1 8.8 %cache_pages.1 = bf16[16,2,128,384]{3,2,1,0:T(8,128)(2,1)} custom-call(s32[18]{0:T(128)S(1)} %pad_add_fusion.meta_ref, bf16[2,5120,384]{2,1,0:T(8,128)(2,1)S(1)} %copy-done), custom_call_target="tpu_custom_call" | custom-call | flops 10000000 | bytes 7000000 | tf_op jit(solution)/shard_map/cache_pages/pallas_call | solution.py:719
  218.8 0.0 copy-start.1
  218.8 0.0 copy-done.3
  218.9 0.8 copy.18
  219.6 0.0 copy-done.2
  219.6 0.9 copy.19
  220.5 0.3 copy-done.1
  220.8 1.4 copy.20
  (4 shorter events, 0.0 us)
Async XLA Ops:
  206.8 3.2 %copy-start = (bf16[2,5120,384]{2,1,0:T(8,128)(2,1)S(1)}, bf16[2,5120,384]{2,1,0:T(8,128)(2,1)}, u32[]{:S(2)}) copy-start(bf16[2,5120,384]{2,1,0:T(8,128)(2,1)} %get-tuple-element.13.kv_hbm) | copy-start | bytes 23592964
  210.0 8.8 %copy-start.3 = (bf16[320,640]{1,0:T(8,128)(2,1)S(1)}, bf16[320,640]{1,0:T(8,128)(2,1)}, u32[]{:S(2)}) copy-start(bf16[320,640]{1,0:T(8,128)(2,1)} %get-tuple-element.29) | copy-start | bytes 1228804
  210.1 9.6 %copy-start.2 = (bf16[3,8,40,384]{3,2,1,0:T(8,128)(2,1)S(1)}, bf16[3,8,40,384]{3,2,1,0:T(8,128)(2,1)}, u32[]{:S(2)}) copy-start(bf16[3,8,40,384]{3,2,1,0:T(8,128)(2,1)} %get-tuple-element.31) | copy-start | bytes 2211844
  218.8 1.9 copy-start.1

commit v4 on v3

--- a/solution.py
+++ b/solution.py
@@ -17,15 +17,6 @@
 norm_epsilon = 1e-06
 rope_theta = 500000.0
 big_negative = -1e30
-
-
-def locate_tokens(token_index, lengths):
-    prompt_ends = jnp.cumsum(lengths)
-    prompt_starts = prompt_ends - lengths
-    segment = jnp.sum((token_index[:, None] >= prompt_ends[None, :]).astype(jnp.int32), axis=1)
-    onehot = segment[:, None] == jnp.arange(lengths.shape[0], dtype=jnp.int32)[None, :]
-    start = jnp.sum(jnp.where(onehot, prompt_starts[None, :], 0), axis=1)
-    return start
 
 
 ALIGN = 16
@@ -78,86 +69,67 @@
     def __init__(self, me, src, stages, send, recv):
         self.me, self.src, self.stages, self.send, self.recv = me, src, stages, send, recv
 
-    def go(self, away, stage, number, slot, src, device):
-        dst, recv = self.stages[stage].at[slot], self.recv.at[stage, slot]
-
-        @pl.when(away)
-        def _():
-            rdma(src, dst, self.send.at[stage, number], recv, device).start()
-
-        @pl.when(jnp.logical_not(away))
-        def _():
+    def go(self, i, stage, slot, src, dst, device):
+        recv = self.recv.at[stage, slot]
+        if i == 0:
             pltpu.make_async_copy(src, dst, recv).start()
-
-    def got(self, stage, slot):
-        arrived(
-            self.stages[stage].at[slot], self.recv.at[stage, slot], self.send.at[stage, 0],
-            self.me.here,
-        )
+        else:
+            rdma(src, dst, self.send.at[stage, i], recv, device).start()
+
+    def to(self, stage, slot):
+        if stage == 0:
+            return self.stages[0].at[slot // 4, lax.rem(slot // 2, 2), lax.rem(slot, 2)]
+        if stage == 1:
+            return self.stages[1].at[slot // 2, lax.rem(slot, 2)]
+        return self.stages[2].at[slot]
+
+    def got(self, stage, count):
+        for slot in range(count):
+            arrived(
+                self.to(stage, slot), self.recv.at[stage, slot], self.send.at[stage, 0],
+                self.me.here,
+            )
 
     def first(self):
         me = self.me
-
-        def send(i):
-            dx, dk, zh = i // 4, lax.rem(i // 2, 2), lax.rem(i, 2)
-            x, core = lax.rem(me.x + dx, 4), lax.rem(me.core + dk, 2)
-            device = me.at(x=x, core=core)
-            slot = (me.x * 2 + me.core) * 2 + zh
-            self.go(i >= 2, 0, i, slot, self.src.at[zh * 8 + 2 * x + core], device)
-
-        each(16, send)
+        slot = me.x * 2 + me.core
+        for i in (3, 5, 2, 7, 4, 6, 1, 0):
+            x, core = lax.rem(me.x + i // 2, 4), lax.rem(me.core + i, 2)
+            self.go(
+                i, 0, slot, self.src.at[:, x * 2 + core], self.to(0, slot), me.at(x=x, core=core)
+            )
 
     def second(self):
         me = self.me
-
-        def send(i):
-            dx, ks, zh = i // 4, lax.rem(i // 2, 2), lax.rem(i, 2)
-            xs = wrap(me.x - dx, 4)
-            came = (xs * 2 + ks) * 2 + zh
-            self.got(0, came)
-            zl = lax.rem(xs, 2)
-            away = jnp.logical_or(zl != me.zl, zh != me.zh)
-            slot = ((me.zh * 2 + me.zl) * 2 + xs // 2) * 2 + ks
-            self.go(away, 1, came, slot, self.stages[0].at[came], me.at(zl=zl, zh=zh))
-
-        each(16, send)
+        self.got(0, 8)
+        slot = me.zh * 2 + me.zl
+        for i in (2, 1, 3, 0):
+            z = lax.rem(slot + i, 4)
+            zh, zl = z // 2, lax.rem(z, 2)
+            self.go(
+                i, 1, slot, self.stages[0].at[:, zl, :, zh], self.to(1, slot), me.at(zh=zh, zl=zl)
+            )
 
     def third(self):
         me = self.me
-
-        def send(i):
-            zs = lax.rem(me.zh * 2 + me.zl + i // 4, 4)
-            xh, ks = lax.rem(i // 2, 2), lax.rem(i, 2)
-            came = (zs * 2 + xh) * 2 + ks
-            self.got(1, came)
-            y = (zs // 2) * 2 + xh
-            slot = ks * 8 + me.y * 2 + lax.rem(zs, 2)
-            self.go(y != me.y, 2, came, slot, self.stages[1].at[came], me.at(y=y))
-
-        each(16, send)
+        self.got(1, 4)
+        for i in (2, 1, 3, 0):
+            y = lax.rem(me.y + i, 4)
+            self.go(
+                i, 2, me.y, self.stages[1].at[y // 2, :, lax.rem(y, 2)], self.to(2, me.y),
+                me.at(y=y),
+            )
 
     def last(self):
-        each(16, lambda i: self.got(2, i))
+        self.got(2, 4)
 
     def drain(self):
-        me = self.me
-
-        def sent(away, stage, number):
-            @pl.when(away)
-            def _():
+        for stage, count in ((0, 8), (1, 4), (2, 4)):
+            for i in range(1, count):
+                ref = self.to(stage, 0)
                 rdma(
-                    self.src.at[0], self.src.at[0], self.send.at[stage, number],
-                    self.recv.at[stage, 0], me.here,
+                    ref, ref, self.send.at[stage, i], self.recv.at[stage, 0], self.me.here
                 ).wait_send()
-
-        def each_piece(i):
-            sent(i >= 2, 0, i)
-            xs, zh = i // 4, lax.rem(i, 2)
-            sent(jnp.logical_or(lax.rem(xs, 2) != me.zl, zh != me.zh), 1, i)
-            zs, xh = i // 4, lax.rem(i // 2, 2)
-            sent((zs // 2) * 2 + xh != me.y, 2, i)
-
-        each(16, each_piece)
 
 
 class Gather:
@@ -281,7 +253,7 @@
     for j in range(3):
         turned = qkv_ref[j].T
         for c in range(n_col):
-            qsrc[c, j] = turned[c * fine:(c + 1) * fine, :].astype(bf16)
+            qsrc[c // 8, c % 8, j] = turned[c * fine:(c + 1) * fine, :].astype(bf16)
     pl.semaphore_wait(barrier, 7 + 3 + n_row - 1)
 
     qkv = Relay(me, qsrc, (q1, q2, q3), q_send, q_recv)
@@ -291,15 +263,17 @@
         fetch(j).wait()
         turned = gf32[j].T
         for c in range(n_col):
-            gsrc[c, j] = turned[c * fine:(c + 1) * fine, :].astype(bf16)
+            gsrc[c // 8, c % 8, j] = turned[c * fine:(c + 1) * fine, :].astype(bf16)
+    gate.first()
     qkv.second()
-    gate.first()
     qkv.third()
     qkv.last()
 
+    depth = w_all.shape[2] // 4
+
     def join(stage, r, j):
         return jnp.concatenate(
-            [stage[r, j].astype(f32), stage[n_row + r, j].astype(f32)], axis=1
+            [stage[r // 2, r % 2, 0, j].astype(f32), stage[r // 2, r % 2, 1, j].astype(f32)], axis=1
         )
 
     for j in range(3):
@@ -308,10 +282,15 @@
             qblk_ref[j, 2 * pair] = first.astype(bf16)
             qblk_ref[j, 2 * pair + 1] = second.astype(bf16)
             both = jnp.concatenate([first, second], axis=0).astype(bf16)
-            w_all[me.chip, core, j, pair * 2 * fine:(pair + 1) * 2 * fine, :] = both
-
-    depth = w_all.shape[3] // 2
-    weights = Gather(me, True, lambda p, k, h: w_all.at[p, k, :, h * depth:(h + 1) * depth, :], w_send, w_recv)
+            at = pl.multiple_of(core * depth * 2 + pair * 2 * fine, 16)
+            w_all[me.chip, j, pl.ds(at, 2 * fine), :] = both
+
+
+    def weight_rows(chip, of_core, half):
+        at = pl.multiple_of((of_core * 2 + half) * depth, 16)
+        return w_all.at[chip, :, pl.ds(at, depth), :]
+
+    weights = Gather(me, True, weight_rows, w_send, w_recv)
     weights.start(0)
     weights.start(1)
 
@@ -352,40 +331,44 @@
     )
     own_o.start()
 
-    def part(c):
+    def part(chip):
         return jnp.concatenate(
             [
-                hid_ref[:, r * width_row + c * fine:r * width_row + (c + 1) * fine].astype(f32)
+                hid_ref[:, r * width_row + c * fine:r * width_row + (c + 1) * fine]
+                for c in (2 * chip, 2 * chip + 1)
                 for r in range(n_row)
             ],
             axis=1,
-        ).astype(bf16)
-
-    for c in range(n_col):
-        hid_parts[c] = part(c)
-
-    gate.second()
+        )
+
+    for chip in range(n_col // 2):
+        hid_parts[chip] = part(chip)
+
+    for j in range(3):
+        proj_ref[j] = jnp.zeros_like(proj_ref[j])
+
+    def project(dz, dx):
+        weights.sibling(dz, dx)
+        chip = weights.block(dz, dx)
+        for j in range(3):
+            proj_ref[j] += jnp.dot(hid_parts[chip], w_all[chip, j], preferred_element_type=f32)
+
     weights.z_turn()
     each(n_row - 1, lambda i: o_copy(i).start())
     weights.x_turn(0)
+    gate.second()
     weights.x_turn(1)
+    project(0, 0)
+    project(1, 0)
+    project(0, -1)
+    project(0, 1)
+    weights.x_end(0)
     gate.third()
-    weights.x_end(0)
+    project(1, -1)
+    project(1, 1)
     weights.x_end(1)
-
-    for j in range(3):
-        proj_ref[j] = jnp.zeros_like(proj_ref[j])
-
-    def project(chip, of_core):
-        lhs = hid_parts[2 * chip + of_core]
-        for j in range(3):
-            proj_ref[j] += jnp.dot(lhs, w_all[chip, of_core, j], preferred_element_type=f32)
-
-    each(n_col // 2, lambda chip: project(chip, core))
-    for dz in range(2):
-        for dx in (0, -1, 1, 2):
-            weights.sibling(dz, dx)
-    each(n_col // 2, lambda chip: project(chip, 1 - core))
+    project(0, 2)
+    project(1, 2)
 
     def o_relay(i):
         of_row = lax.rem(row + n_row - 1 - i, n_row)
@@ -399,7 +382,8 @@
         for j in range(2):
             gblk_ref[j, r] = join(g3, r, j).astype(bf16)
 
-    each(n_row, g_join)
+    for r in range(n_row):
+        g_join(r)
     each(n_row - 1, lambda i: o_arrived(lax.rem(row + 1 + i, n_row), 1 - core))
     own_o.wait()
     qkv.drain()
@@ -418,8 +402,14 @@
     bf16, f32 = jnp.bfloat16, jnp.float32
     dma = pltpu.SemaphoreType.DMA
     vmem, anywhere = pl.BlockSpec(memory_space=pltpu.VMEM), pl.BlockSpec(memory_space=pl.ANY)
-    q_piece = pltpu.VMEM((n_col, 3, fine, part), bf16)
-    g_piece = pltpu.VMEM((n_col, 2, fine, gate_part), bf16)
+    def pieces(*shape):
+        return [
+            pltpu.VMEM((2, n_col // 2) + shape, bf16),
+            pltpu.VMEM((2, 2, 2, 2) + shape, bf16),
+            pltpu.VMEM((2, 2, 2, 2) + shape, bf16),
+            pltpu.VMEM((4, 2, 2) + shape, bf16),
+        ]
+
     return pl.pallas_call(
         functools.partial(sync_body, n_row=n_row, n_col=n_col),
         out_shape=(
@@ -431,15 +421,15 @@
         in_specs=[vmem, anywhere, vmem, anywhere],
         out_specs=(vmem, vmem, vmem, anywhere),
         scratch_shapes=[
-            pltpu.VMEM((n_col, tok, n_row * fine), bf16),
-            q_piece, q_piece, q_piece, q_piece,
-            pltpu.VMEM((n_col // 2, 2, 3, n_row * fine, width), bf16),
+            pltpu.VMEM((n_col // 2, tok, 2 * n_row * fine), bf16),
+            *pieces(3, fine, part),
+            pltpu.VMEM((n_col // 2, 3, 2 * n_row * fine, width), bf16),
             pltpu.VMEM((2, gate_part, row_width), f32),
-            g_piece, g_piece, g_piece, g_piece,
-            dma((3, n_col)),
-            dma((3, n_col)),
-            dma((3, n_col)),
-            dma((3, n_col)),
+            *pieces(2, fine, gate_part),
+            dma((3, 8)),
+            dma((3, 8)),
+            dma((3, 8)),
+            dma((3, 8)),
             dma((n_col // 2, 2, 4)),
             dma((n_col // 2, 2, 2)),
             dma((n_row,)),
@@ -473,7 +463,7 @@
 
 
 def layer_body(
-    proj_ref, cos_ref, sin_ref, gain_ref, start_ref, ocol_ref, post_ref, hid_hbm,
+    lengths_ref, proj_ref, cos_ref, sin_ref, gain_ref, ocol_ref, post_ref, hid_hbm,
     out_ref, kv_out,
     query, kv, mixed_all, residual, sq_in, sq_out,
     kv_send, kv_recv, a_send, a_recv, s_send, s_recv, t_send, t_recv, local_sem,
@@ -574,7 +564,12 @@
     first_key = pl.multiple_of(jnp.maximum(col - reach, 0) * tok, 64)
     query_index = col * tok + lax.broadcasted_iota(jnp.int32, (tok, 1), 0)
     key_index = first_key + lax.broadcasted_iota(jnp.int32, (1, span), 1)
-    allowed = (key_index <= query_index) & (key_index >= start_ref[...])
+    prompt_start = jnp.zeros((tok, 1), jnp.int32)
+    end = 0
+    for p in range(lengths_ref.shape[0]):
+        end = end + lengths_ref[p]
+        prompt_start = jnp.where(query_index >= end, end, prompt_start)
+    allowed = (key_index <= query_index) & (key_index >= prompt_start)
     for head in range(heads):
         lanes = slice(head * HD, (head + 1) * HD)
         keys = kv[0, pl.ds(first_key, span), lanes]
@@ -638,13 +633,13 @@
     for at in range(0, out_width, 128):
         lanes = slice(at, at + 128)
         out_ref[:, lanes] = (
-            residual[:, lanes].astype(f32) + product[:, lanes] * scale * post_ref[:, lanes]
+            residual[:, lanes].astype(f32) + product[:, lanes] * scale * post_ref[at // 128:at // 128 + 1, :]
         ).astype(bf16)
     each(n_row - 1, lambda i: share(sq_out, t_send, t_recv, i).wait_send())
     give.wait()
 
 
-def attention_layer(projected, cosine, sine, gain, start, o_columns, post, hidden, n_row, n_col):
+def attention_layer(lengths, projected, cosine, sine, gain, o_columns, post, hidden, n_row, n_col):
     _, tok, width = projected.shape
     out_width = o_columns.shape[1]
     bf16, f32 = jnp.bfloat16, jnp.float32
@@ -656,7 +651,7 @@
             jax.ShapeDtypeStruct((tok, out_width), bf16),
             jax.ShapeDtypeStruct((2, n_col * tok, width), bf16),
         ),
-        in_specs=[vmem] * 7 + [anywhere],
+        in_specs=[pl.BlockSpec(memory_space=pltpu.SMEM)] + [vmem] * 6 + [anywhere],
         out_specs=(vmem, anywhere),
         scratch_shapes=[
             pltpu.VMEM((tok, width), bf16),
@@ -682,53 +677,63 @@
             flops=8_000_000_000, bytes_accessed=20_000_000, transcendentals=3_000_000
         ),
         name="attention_layer",
-    )(projected, cosine, sine, gain, start, o_columns, post, hidden)
-
-
-def cache_body(meta_ref, kv_hbm, out_ref, windows, sems):
+    )(lengths, projected, cosine, sine, gain, o_columns, post, hidden)
+
+
+def cache_body(lengths_ref, owner_ref, table_ref, kv_hbm, out_ref, windows, sems):
     tokens = kv_hbm.shape[1]
-    begin, length = meta_ref[0], meta_ref[1]
-
-    def locate(slot):
-        first = jnp.minimum(begin + meta_ref[2 + slot] * PAGE, tokens - 1)
+    col = lax.axis_index("col")
+    begin = length = mine = end = 0
+    for p in range(lengths_ref.shape[0]):
+        here = owner_ref[p] == col
+        begin, length = jnp.where(here, end, begin), jnp.where(here, lengths_ref[p], length)
+        mine = jnp.where(here, p, mine)
+        end = end + lengths_ref[p]
+
+    def locate(page):
+        first = jnp.minimum(begin + page * PAGE, tokens - 1)
         base = pl.multiple_of(jnp.minimum((first // ALIGN) * ALIGN, tokens - WINDOW), ALIGN)
         return first, base
 
-    def fetch(slot):
-        _, base = locate(slot)
+    def fetch(page):
+        _, base = locate(page)
         return pltpu.make_async_copy(
-            kv_hbm.at[:, pl.ds(base, WINDOW), :], windows.at[slot], sems.at[slot]
-        )
-
-    each(PAGES, lambda slot: fetch(slot).start())
-
-    def place(slot):
-        fetch(slot).wait()
-        first, base = locate(slot)
-        turn = lax.rem(WINDOW - (first - base), WINDOW)
-        rows = lax.broadcasted_iota(jnp.int32, (PAGE, 1), 0) + meta_ref[2 + slot] * PAGE
+            kv_hbm.at[:, pl.ds(base, WINDOW), :], windows.at[page], sems.at[page]
+        )
+
+    each(PAGES, lambda page: fetch(page).start())
+
+    def place(page):
+        fetch(page).wait()
+        first, base = locate(page)
+        row = lax.broadcasted_iota(jnp.int32, (PAGE, WINDOW), 0)
+        source = lax.broadcasted_iota(jnp.int32, (PAGE, WINDOW), 1)
+        pick = (row + (first - base) == source) & (row + page * PAGE < length)
+        pick = pick.astype(jnp.float32).astype(jnp.bfloat16)
+        slot = table_ref[mine, page]
         for part in range(2):
-            piece = pltpu.roll(windows[slot, part].astype(jnp.float32), turn, 0)[:PAGE]
-            out_ref[slot, part] = jnp.where(rows < length, piece, 0.0).astype(jnp.bfloat16)
+            moved = jnp.dot(pick, windows[page, part], preferred_element_type=jnp.float32)
+            out_ref[slot, part] = moved.astype(jnp.bfloat16)
 
     each(PAGES, place)
 
 
-def build_cache(meta, kv):
+def build_cache(lengths, owner, page_table, kv):
     width = kv.shape[2]
+    smem = pl.BlockSpec(memory_space=pltpu.SMEM)
     return pl.pallas_call(
         cache_body,
         out_shape=jax.ShapeDtypeStruct((PAGES, 2, PAGE, width), jnp.bfloat16),
-        in_specs=[pl.BlockSpec(memory_space=pltpu.SMEM), pl.BlockSpec(memory_space=pl.ANY)],
+        in_specs=[smem, smem, smem, pl.BlockSpec(memory_space=pl.ANY)],
         out_specs=pl.BlockSpec(memory_space=pltpu.VMEM),
         scratch_shapes=[
             pltpu.VMEM((PAGES, 2, WINDOW, width), jnp.bfloat16),
             pltpu.SemaphoreType.DMA((PAGES,)),
         ],
-        compiler_params=pltpu.CompilerParams(vmem_limit_bytes=16 << 20),
+        compiler_params=pltpu.CompilerParams(vmem_limit_bytes=60 << 20),
         cost_estimate=pl.CostEstimate(flops=10_000_000, bytes_accessed=7_000_000, transcendentals=0),
         name="cache_pages",
-    )(meta, kv)
+    )(lengths, owner, page_table, kv)
 
 
 def local(
@@ -742,7 +747,11 @@
         qkv_train, gate_up_train, hidden, o_weight, n_row, n_col
     )
     token_index = col_index * tok_rows + jnp.arange(tok_rows, dtype=jnp.int32)
-    token_start = locate_tokens(token_index, lengths)
+    token_start = jnp.zeros_like(token_index)
+    end = 0
+    for p in range(lengths.shape[0]):
+        end = end + lengths[p]
+        token_start = jnp.where(token_index >= end, end, token_start)
     half_dim = HD // 2
     frequency = rope_theta ** (-2.0 * jnp.arange(half_dim, dtype=jnp.float32) / HD)
     angles = (token_index - token_start).astype(jnp.float32)[:, None] * frequency[None, :]
@@ -750,21 +759,11 @@
     cosine = jnp.concatenate([cosine, cosine], axis=1)
     sine = jnp.concatenate([-sine, sine], axis=1)
 
-    prompt_starts = jnp.cumsum(lengths) - lengths
-    owned = owner == col_index
-    my_start = jnp.sum(jnp.where(owned, prompt_starts, 0))
-    my_length = jnp.sum(jnp.where(owned, lengths, 0))
-    my_pages = jnp.sum(jnp.where(owned[:, None], page_table, 0), axis=0)
-    slots = jnp.arange(PAGES, dtype=jnp.int32)
-    page_of = jnp.sum(jnp.where(my_pages[None, :] == slots[:, None], slots[None, :], 0), axis=1)
-    page_of = jnp.where(my_length > 0, page_of, slots)
-    meta = jnp.concatenate([jnp.stack([my_start, my_length]), page_of]).astype(jnp.int32)
-
     layer_out, kv = attention_layer(
-        projected, cosine, sine, qk_gain, token_start[:, None], o_columns,
-        post_gain[None, :], hidden, n_row, n_col,
-    )
-    cache_pages = build_cache(meta, kv)
+        lengths, projected, cosine, sine, qk_gain, o_columns,
+        post_gain.reshape(-1, 128), hidden, n_row, n_col,
+    )
+    cache_pages = build_cache(lengths, owner, page_table, kv)
     return (layer_out, cache_pages[None], weight_blocks, gate_up_blocks)
 
 

time: 223 us -> 228 us (1.022)
  Pallas kernels: 206 us -> 218 us
  other arithmetic: 6.13 us -> 2.19 us
  local copies, waits for them, and re-layouts: 8.55 us -> 4.68 us
    pallas_call x1, Pallas kernels: 120 us -> 142 us  [sync_weights(): pl.pallas_call(functools.partial(sync_body, n_row=n_row, n_col=n_col), ou...]
    pallas_call x1, Pallas kernels: 77.8 us -> 68.8 us  [attention_layer(): pl.pallas_call(functools.partial(layer_body, n_row=n_row, n_col=n_col), o...]
    unnamed x11 -> x9, local copies, waits for them, and re-layouts: 6.51 us -> 3.29 us
    reduce_sum x5 -> x0, other arithmetic: 2.38 us -> none  [the longest x1 1.32 us: local(): my_start = jnp.sum(jnp.where(owned, prompt_starts, 0))]
where the time goes in v4:
time: 228 us
  Pallas kernels  218 us (96%)
  local copies, waits for them, and re-layouts  4.68 us (2%)
  between operations  3.31 us (1%)
    pallas_call x1, Pallas kernels, sync_weights(): pl.pallas_call(functools.partial(sync_body, n_row=n_row, n_col=n_col), ou...  142 us
    pallas_call x1, Pallas kernels, attention_layer(): pl.pallas_call(functools.partial(layer_body, n_row=n_row, n_col=n_col), o...  68.8 us
    pallas_call x1, Pallas kernels, build_cache(): pl.pallas_call(cache_body, out_shape=jax.ShapeDtypeStruct((PAGES, 2, PAGE...  7.23 us

profile of v4, /device:TPU:0, one launch (start us, length us, event | category | flops | bytes accessed | tf_op | source)
XLA Modules:
  0.0 227.9 jit_solution(1376717118104968452)
XLA Ops:
  0.6 1.4 fusion.5
  4.6 0.7 subtract_convert_fusion
  5.3 0.6 fusion
  6.0 0.9 pad_maximum_fusion
  6.8 141.7 %sync_weights.1 = (f32[3,320,384]{2,1,0:T(8,128)}, bf16[3,8,40,384]{3,2,1,0:T(8,128)(2,1)}, bf16[2,8,40,1728]{3,2,1,0:T(8,128)(2,1)}, bf16[3072,640]{1,0:T(8,128)(2,1)}) custom-call(f32[3,192,640]{2,1,0:T(8,128)} %bitcast.10, f32[2,864,640]{2,1,0:T(8,128)} %bitcast.9, bf16[320,5120]{1,0:T(8,128)(2,1)} %hid_hbm.1, bf16[384,5120]{1,0:T(8,128)(2,1)} %ow_hbm.1), custom_call_target="tpu_custom_call" | custom-call | flops 3774873600 | bytes 30000000 | tf_op jit(solution)/shard_map/sync_weights/pallas_call | solution.py:413
  148.5 68.8 %attention_layer.1 = (bf16[320,640]{1,0:T(8,128)(2,1)}, bf16[2,5120,384]{2,1,0:T(8,128)(2,1)}) custom-call(s32[4]{0:T(128)} %lengths_ref.3, f32[3,320,384]{2,1,0:T(8,128)} %get-tuple-element.10.proj_ref, f32[320,128]{1,0:T(8,128)} %get-tuple-element.23.cos_ref, f32[320,128]{1,0:T(8,128)} %get-tuple-element.24.sin_ref, f32[2,384]{1,0:T(2,128)} %gain_ref.1, ...), custom_call_target="tpu_custom_call" | custom-call | flops 8000000000 | bytes 20000000 | tf_op jit(solution)/shard_map/attention_layer/pallas_call | solution.py:648
  217.3 0.0 copy-start.2
  217.3 0.0 copy-start.1
  217.4 7.2 %cache_pages.1 = bf16[16,2,128,384]{3,2,1,0:T(8,128)(2,1)} custom-call(s32[4]{0:T(128)} %lengths_ref.3, s32[4]{0:T(128)} %owner_ref.1, s32[4,16]{1,0:T(4,128)} %table_ref.1, bf16[2,5120,384]{2,1,0:T(8,128)(2,1)} %get-tuple-element.13.kv_hbm), custom_call_target="tpu_custom_call" | custom-call | flops 10000000 | bytes 7000000 | tf_op jit(solution)/shard_map/cache_pages/pallas_call | solution.py:724
  224.6 0.0 copy-start
  224.6 0.0 copy-done.2
  224.6 0.8 copy.16
  225.4 0.0 copy-done.1
  225.4 0.9 copy.17
  226.2 0.3 copy-done
  226.5 1.4 copy.18
  (1 shorter events, 0.0 us)
Async XLA Ops:
  217.3 7.3 %copy-start.2 = (bf16[320,640]{1,0:T(8,128)(2,1)S(1)}, bf16[320,640]{1,0:T(8,128)(2,1)}, u32[]{:S(2)}) copy-start(bf16[320,640]{1,0:T(8,128)(2,1)} %get-tuple-element.29) | copy-start | bytes 1228804
  217.3 8.0 %copy-start.1 = (bf16[3,8,40,384]{3,2,1,0:T(8,128)(2,1)S(1)}, bf16[3,8,40,384]{3,2,1,0:T(8,128)(2,1)}, u32[]{:S(2)}) copy-start(bf16[3,8,40,384]{3,2,1,0:T(8,128)(2,1)} %get-tuple-element.31) | copy-start | bytes 2211844
  224.6 1.9 copy-start

commit v5 on v4

--- a/solution.py
+++ b/solution.py
@@ -65,71 +65,112 @@
     pl.semaphore_signal(sem, inc=1, device_id=device, device_id_type=pl.DeviceIdType.MESH)
 
 
+def near_first(step):
+    return step + (step // 2) * (1 - 2 * lax.rem(step, 2))
+
+
 class Relay:
     def __init__(self, me, src, stages, send, recv):
         self.me, self.src, self.stages, self.send, self.recv = me, src, stages, send, recv
 
-    def go(self, i, stage, slot, src, dst, device):
-        recv = self.recv.at[stage, slot]
-        if i == 0:
-            pltpu.make_async_copy(src, dst, recv).start()
-        else:
-            rdma(src, dst, self.send.at[stage, i], recv, device).start()
-
-    def to(self, stage, slot):
-        if stage == 0:
-            return self.stages[0].at[slot // 4, lax.rem(slot // 2, 2), lax.rem(slot, 2)]
-        if stage == 1:
-            return self.stages[1].at[slot // 2, lax.rem(slot, 2)]
-        return self.stages[2].at[slot]
-
-    def got(self, stage, count):
-        for slot in range(count):
+    def go(self, away, stage, number, slot, src, device):
+        dst = self.stages[stage].at[slot]
+
+        @pl.when(away)
+        def _():
+            rdma(src, dst, self.send.at[stage, number], self.recv.at[stage, slot], device).start()
+
+        @pl.when(jnp.logical_not(away))
+        def _():
+            dst[...] = src[...]
+
+    def got(self, away, stage, slot):
+        @pl.when(away)
+        def _():
             arrived(
-                self.to(stage, slot), self.recv.at[stage, slot], self.send.at[stage, 0],
+                self.stages[stage].at[slot], self.recv.at[stage, slot], self.send.at[stage, 0],
                 self.me.here,
             )
 
     def first(self):
         me = self.me
-        slot = me.x * 2 + me.core
-        for i in (3, 5, 2, 7, 4, 6, 1, 0):
-            x, core = lax.rem(me.x + i // 2, 4), lax.rem(me.core + i, 2)
-            self.go(
-                i, 0, slot, self.src.at[:, x * 2 + core], self.to(0, slot), me.at(x=x, core=core)
-            )
+
+        def send(i):
+            dx, dk, zh = 3 - i // 4, lax.rem(i // 2, 2), lax.rem(i, 2)
+            x, core = lax.rem(me.x + near_first(dx), 4), lax.rem(me.core + dk, 2)
+            slot = (me.x * 2 + me.core) * 2 + zh
+            away = jnp.logical_or(dx > 0, dk > 0)
+            self.go(away, 0, i, slot, self.src.at[zh * 8 + 2 * x + core], me.at(x=x, core=core))
+
+        each(16, send)
 
     def second(self):
         me = self.me
-        self.got(0, 8)
-        slot = me.zh * 2 + me.zl
-        for i in (2, 1, 3, 0):
-            z = lax.rem(slot + i, 4)
-            zh, zl = z // 2, lax.rem(z, 2)
-            self.go(
-                i, 1, slot, self.stages[0].at[:, zl, :, zh], self.to(1, slot), me.at(zh=zh, zl=zl)
-            )
-
-    def third(self):
+
+        def send(i):
+            ks, zh = lax.rem(i // 2, 2), lax.rem(i, 2)
+            xs = wrap(me.x - near_first(i // 4), 4)
+            came = (xs * 2 + ks) * 2 + zh
+            self.got(jnp.logical_or(i >= 4, ks != me.core), 0, came)
+            zl = lax.rem(xs, 2)
+            away = jnp.logical_or(zl != me.zl, zh != me.zh)
+            slot = ((me.zh * 2 + me.zl) * 2 + xs // 2) * 2 + ks
+            self.go(away, 1, came, slot, self.stages[0].at[came], me.at(zl=zl, zh=zh))
+
+        each(16, send)
+
+    def third(self, wait=True):
         me = self.me
-        self.got(1, 4)
-        for i in (2, 1, 3, 0):
-            y = lax.rem(me.y + i, 4)
-            self.go(
-                i, 2, me.y, self.stages[1].at[y // 2, :, lax.rem(y, 2)], self.to(2, me.y),
-                me.at(y=y),
-            )
+
+        def send(i):
+            zs = lax.rem(me.zh * 2 + me.zl + near_first(i // 4), 4)
+            xh, ks = lax.rem(i // 2, 2), lax.rem(i, 2)
+            came = (zs * 2 + xh) * 2 + ks
+            if wait:
+                self.got(i >= 4, 1, came)
+            y = (zs // 2) * 2 + xh
+            slot = (me.y * 2 + lax.rem(zs, 2)) * 2 + ks
+            self.go(y != me.y, 2, came, slot, self.stages[1].at[came], me.at(y=y))
+
+        each(16, send)
+
+    def second_last(self):
+        me = self.me
+        each(16, lambda i: self.got(i // 4 != me.zh * 2 + me.zl, 1, i))
 
     def last(self):
-        self.got(2, 4)
-
-    def drain(self):
-        for stage, count in ((0, 8), (1, 4), (2, 4)):
-            for i in range(1, count):
-                ref = self.to(stage, 0)
+        each(16, lambda i: self.got(i // 4 != self.me.y, 2, i))
+
+    def drain(self, stages=(0, 1, 2)):
+        me = self.me
+
+        def sent(away, stage, number):
+            if stage not in stages:
+                return
+
+            @pl.when(away)
+            def _():
                 rdma(
-                    ref, ref, self.send.at[stage, i], self.recv.at[stage, 0], self.me.here
+                    self.src.at[0], self.src.at[0], self.send.at[stage, number],
+                    self.recv.at[stage, 0], me.here,
                 ).wait_send()
+
+        def each_piece(i):
+            sent(jnp.logical_or(i < 12, lax.rem(i // 2, 2) > 0), 0, i)
+            xs, zh = i // 4, lax.rem(i, 2)
+            sent(jnp.logical_or(lax.rem(xs, 2) != me.zl, zh != me.zh), 1, i)
+            zs, xh = i // 4, lax.rem(i // 2, 2)
+            sent((zs // 2) * 2 + xh != me.y, 2, i)
+
+        each(16, each_piece)
+
+
+def join(stage, r, j, rows, columns):
+    halves = [
+        stage[2 * r + half, j * rows:(j + 1) * rows, :columns].astype(jnp.float32)
+        for half in range(2)
+    ]
+    return jnp.concatenate(halves, axis=1)
 
 
 class Gather:
@@ -225,8 +266,8 @@
 
 def sync_body(
     qkv_ref, gate_hbm, hid_ref, ow_hbm,
-    proj_ref, qblk_ref, gblk_ref, ocol_ref,
-    hid_parts, qsrc, q1, q2, q3, w_all, gf32, gsrc, g1, g2, g3,
+    proj_ref, qblk_ref, g2, ocol_ref,
+    hid_parts, qsrc, q1, q2, q3, w_all, gf32, gsrc, g1,
     q_send, q_recv, g_send, g_recv, w_send, w_recv, o_send, o_fwd, o_recv, local_sem,
     *, n_row, n_col,
 ):
@@ -242,6 +283,15 @@
     for j in range(2):
         fetch(j).start()
 
+    def cut(part, pieces, j):
+        turned = part.T
+        if pieces.shape[2] > part.shape[0]:
+            fill = jnp.zeros((part.shape[1], pieces.shape[2] - part.shape[0]), f32)
+            turned = jnp.concatenate([turned, fill], axis=1)
+        for c in range(n_col):
+            rows = turned[c * fine:(c + 1) * fine, :].astype(bf16)
+            pieces[c, j * fine:(j + 1) * fine, :] = rows
+
     barrier = pltpu.get_barrier_semaphore()
     for i in range(1, 8):
         signal(barrier, me.at(x=lax.rem(me.x + i // 2, 4), core=lax.rem(me.core + i, 2)))
@@ -251,34 +301,25 @@
         signal(barrier, (lax.rem(row + i, n_row), col))
 
     for j in range(3):
-        turned = qkv_ref[j].T
-        for c in range(n_col):
-            qsrc[c // 8, c % 8, j] = turned[c * fine:(c + 1) * fine, :].astype(bf16)
+        cut(qkv_ref[j], qsrc, j)
     pl.semaphore_wait(barrier, 7 + 3 + n_row - 1)
 
     qkv = Relay(me, qsrc, (q1, q2, q3), q_send, q_recv)
-    gate = Relay(me, gsrc, (g1, g2, g3), g_send, g_recv)
+    gate = Relay(me, gsrc, (g1, g2), g_send, g_recv)
     qkv.first()
     for j in range(2):
         fetch(j).wait()
-        turned = gf32[j].T
-        for c in range(n_col):
-            gsrc[c // 8, c % 8, j] = turned[c * fine:(c + 1) * fine, :].astype(bf16)
+        cut(gf32[j], gsrc, j)
+    qkv.second()
     gate.first()
-    qkv.second()
     qkv.third()
     qkv.last()
 
     depth = w_all.shape[2] // 4
 
-    def join(stage, r, j):
-        return jnp.concatenate(
-            [stage[r // 2, r % 2, 0, j].astype(f32), stage[r // 2, r % 2, 1, j].astype(f32)], axis=1
-        )
-
     for j in range(3):
         for pair in range(n_row // 2):
-            first, second = join(q3, 2 * pair, j), join(q3, 2 * pair + 1, j)
+            first, second = (join(q3, 2 * pair + i, j, fine, qkv_ref.shape[1]) for i in range(2))
             qblk_ref[j, 2 * pair] = first.astype(bf16)
             qblk_ref[j, 2 * pair + 1] = second.astype(bf16)
             both = jnp.concatenate([first, second], axis=0).astype(bf16)
@@ -353,20 +394,19 @@
         for j in range(3):
             proj_ref[j] += jnp.dot(hid_parts[chip], w_all[chip, j], preferred_element_type=f32)
 
+    gate.second()
     weights.z_turn()
     each(n_row - 1, lambda i: o_copy(i).start())
     weights.x_turn(0)
-    gate.second()
+    project(0, 0)
     weights.x_turn(1)
-    project(0, 0)
     project(1, 0)
+    weights.x_end(0)
     project(0, -1)
     project(0, 1)
-    weights.x_end(0)
-    gate.third()
+    weights.x_end(1)
     project(1, -1)
     project(1, 1)
-    weights.x_end(1)
     project(0, 2)
     project(1, 2)
 
@@ -376,18 +416,11 @@
         o_forward(of_row).start()
 
     each(n_row - 1, o_relay)
-    gate.last()
-
-    def g_join(r):
-        for j in range(2):
-            gblk_ref[j, r] = join(g3, r, j).astype(bf16)
-
-    for r in range(n_row):
-        g_join(r)
+    gate.second_last()
     each(n_row - 1, lambda i: o_arrived(lax.rem(row + 1 + i, n_row), 1 - core))
     own_o.wait()
     qkv.drain()
-    gate.drain()
+    gate.drain((0, 1))
     weights.drain()
     each(n_row - 1, lambda i: o_copy(i).wait_send())
     each(n_row - 1, lambda i: o_forward(lax.rem(row + 1 + i, n_row)).wait_send())
@@ -402,34 +435,27 @@
     bf16, f32 = jnp.bfloat16, jnp.float32
     dma = pltpu.SemaphoreType.DMA
     vmem, anywhere = pl.BlockSpec(memory_space=pltpu.VMEM), pl.BlockSpec(memory_space=pl.ANY)
-    def pieces(*shape):
-        return [
-            pltpu.VMEM((2, n_col // 2) + shape, bf16),
-            pltpu.VMEM((2, 2, 2, 2) + shape, bf16),
-            pltpu.VMEM((2, 2, 2, 2) + shape, bf16),
-            pltpu.VMEM((4, 2, 2) + shape, bf16),
-        ]
-
+    gate_tiles = -(-gate_part // 128) * 128
     return pl.pallas_call(
         functools.partial(sync_body, n_row=n_row, n_col=n_col),
         out_shape=(
             jax.ShapeDtypeStruct((3, tok, width), f32),
             jax.ShapeDtypeStruct((3, n_row, fine, width), bf16),
-            jax.ShapeDtypeStruct((2, n_row, fine, 2 * gate_part), bf16),
+            jax.ShapeDtypeStruct((n_col, 2 * fine, gate_tiles), bf16),
             jax.ShapeDtypeStruct((n_row * o_weight.shape[0], width_model // n_row), bf16),
         ),
         in_specs=[vmem, anywhere, vmem, anywhere],
         out_specs=(vmem, vmem, vmem, anywhere),
         scratch_shapes=[
             pltpu.VMEM((n_col // 2, tok, 2 * n_row * fine), bf16),
-            *pieces(3, fine, part),
+            *[pltpu.VMEM((n_col, 3 * fine, part), bf16)] * 4,
             pltpu.VMEM((n_col // 2, 3, 2 * n_row * fine, width), bf16),
             pltpu.VMEM((2, gate_part, row_width), f32),
-            *pieces(2, fine, gate_part),
-            dma((3, 8)),
-            dma((3, 8)),
-            dma((3, 8)),
-            dma((3, 8)),
+            *[pltpu.VMEM((n_col, 2 * fine, gate_tiles), bf16)] * 2,
+            dma((3, n_col)),
+            dma((3, n_col)),
+            dma((2, n_col)),
+            dma((2, n_col)),
             dma((n_col // 2, 2, 4)),
             dma((n_col // 2, 2, 2)),
             dma((n_row,)),
@@ -463,9 +489,9 @@
 
 
 def layer_body(
-    lengths_ref, proj_ref, cos_ref, sin_ref, gain_ref, ocol_ref, post_ref, hid_hbm,
-    out_ref, kv_out,
-    query, kv, mixed_all, residual, sq_in, sq_out,
+    lengths_ref, proj_ref, cos_ref, sin_ref, gain_ref, ocol_ref, post_ref, g2, hid_hbm,
+    out_ref, kv_out, gblk_ref,
+    query, kv, mixed_all, residual, sq_in, sq_out, g3, g_send, g_recv,
     kv_send, kv_recv, a_send, a_recv, s_send, s_recv, t_send, t_recv, local_sem,
     *, n_row, n_col,
 ):
@@ -520,6 +546,9 @@
     gathers = [Gather(me, True, tokens_of, kv_send, kv_recv) for _ in range(2)]
     first_sends = Gather(me, True, tokens_of, kv_send, kv_recv)
     first_sends.start(0)
+
+    gate = Relay(me, g2, (g2, g2, g3), g_send, g_recv)
+    gate.third(wait=False)
 
     squares = shared(sq_in, s_send, s_recv)
     cosine, sine = cos_ref[...], sin_ref[...]
@@ -593,10 +622,18 @@
         for _ in range(2)
     ]
 
+    fine = gblk_ref.shape[2]
+
+    def gate_join(r):
+        for j in range(2):
+            gblk_ref[j, r] = join(g3, r, j, fine, gblk_ref.shape[3] // 2).astype(bf16)
+
     def row_gather(z_first):
         g = row_gathers[0 if z_first else 1]
         g.start(0)
         g.start(1)
+        gate.last()
+        each(n_row, gate_join)
         if z_first:
             g.z_turn()
             g.x_turn(0)
@@ -628,6 +665,7 @@
         row_gathers[which].drain()
 
     by_core(me, drain)
+    gate.drain((2,))
 
     scale = lax.rsqrt(column_of(shared(sq_out, t_send, t_recv), 0) / (n_row * out_width) + norm_epsilon)
     for at in range(0, out_width, 128):
@@ -639,7 +677,7 @@
     give.wait()
 
 
-def attention_layer(lengths, projected, cosine, sine, gain, o_columns, post, hidden, n_row, n_col):
+def attention_layer(lengths, projected, cosine, sine, gain, o_columns, post, gate_pieces, gate_shape, hidden, n_row, n_col):
     _, tok, width = projected.shape
     out_width = o_columns.shape[1]
     bf16, f32 = jnp.bfloat16, jnp.float32
@@ -650,9 +688,10 @@
         out_shape=(
             jax.ShapeDtypeStruct((tok, out_width), bf16),
             jax.ShapeDtypeStruct((2, n_col * tok, width), bf16),
+            jax.ShapeDtypeStruct(gate_shape, bf16),
         ),
-        in_specs=[pl.BlockSpec(memory_space=pltpu.SMEM)] + [vmem] * 6 + [anywhere],
-        out_specs=(vmem, anywhere),
+        in_specs=[pl.BlockSpec(memory_space=pltpu.SMEM)] + [vmem] * 7 + [anywhere],
+        out_specs=(vmem, anywhere, vmem),
         scratch_shapes=[
             pltpu.VMEM((tok, width), bf16),
             pltpu.VMEM((2, n_col * tok, width), bf16),
@@ -660,6 +699,9 @@
             pltpu.VMEM((tok, out_width), bf16),
             pltpu.VMEM((n_row, 8, tok), f32),
             pltpu.VMEM((n_row, 8, tok), f32),
+            pltpu.VMEM(gate_pieces.shape, bf16),
+            dma((3, n_col)),
+            dma((3, n_col)),
             dma((n_col // 2, 2, 4)),
             dma((n_col // 2, 2, 2)),
             dma((n_row, 2, 4)),
@@ -677,7 +719,7 @@
             flops=8_000_000_000, bytes_accessed=20_000_000, transcendentals=3_000_000
         ),
         name="attention_layer",
-    )(lengths, projected, cosine, sine, gain, o_columns, post, hidden)
+    )(lengths, projected, cosine, sine, gain, o_columns, post, gate_pieces, hidden)
 
 
 def cache_body(lengths_ref, owner_ref, table_ref, kv_hbm, out_ref, windows, sems):
@@ -743,7 +785,7 @@
     n_col = lax.axis_size("col")
     col_index = lax.axis_index("col")
     tok_rows = hidden.shape[0]
-    projected, weight_blocks, gate_up_blocks, o_columns = sync_weights(
+    projected, weight_blocks, gate_pieces, o_columns = sync_weights(
         qkv_train, gate_up_train, hidden, o_weight, n_row, n_col
     )
     token_index = col_index * tok_rows + jnp.arange(tok_rows, dtype=jnp.int32)
@@ -759,9 +801,11 @@
     cosine = jnp.concatenate([cosine, cosine], axis=1)
     sine = jnp.concatenate([-sine, sine], axis=1)
 
-    layer_out, kv = attention_layer(
+    _, row_width, gate_part = gate_up_train.shape
+    gate_shape = (2, n_row, row_width // n_col, 2 * gate_part)
+    layer_out, kv, gate_up_blocks = attention_layer(
         lengths, projected, cosine, sine, qk_gain, o_columns,
-        post_gain.reshape(-1, 128), hidden, n_row, n_col,
+        post_gain.reshape(-1, 128), gate_pieces, gate_shape, hidden, n_row, n_col,
     )
     cache_pages = build_cache(lengths, owner, page_table, kv)
     return (layer_out, cache_pages[None], weight_blocks, gate_up_blocks)

time: 228 us -> 211 us (0.925)
  Pallas kernels: 218 us -> 200 us
    pallas_call x1, Pallas kernels: 142 us -> 110 us  [sync_weights(): pl.pallas_call(functools.partial(sync_body, n_row=n_row, n_col=n_col), ou...]
    pallas_call x1, Pallas kernels: 68.8 us -> 82.3 us  [attention_layer(): pl.pallas_call(functools.partial(layer_body, n_row=n_row, n_col=n_col), o...]
where the time goes in v5:
time: 211 us; the launch traced here: 210 us
  Pallas kernels  200 us (95%)
  local copies, waits for them, and re-layouts  4.68 us (2%)
  between operations  3.31 us (2%)
  other arithmetic  2.19 us (1%)
    pallas_call x1, Pallas kernels, sync_weights(): pl.pallas_call(functools.partial(sync_body, n_row=n_row, n_col=n_col), ou...  110 us
    pallas_call x1, Pallas kernels, attention_layer(): pl.pallas_call(functools.partial(layer_body, n_row=n_row, n_col=n_col), o...  82.3 us
    pallas_call x1, Pallas kernels, build_cache(): pl.pallas_call(cache_body, out_shape=jax.ShapeDtypeStruct((PAGES, 2, PAGE...  7.23 us

profile of v5, /device:TPU:0, one launch (start us, length us, event | category | flops | bytes accessed | tf_op | source)
XLA Modules:
  0.0 210.0 jit_solution(16885202675476627703)
XLA Ops:
  0.6 1.4 fusion.5
  4.6 0.7 subtract_convert_fusion
  5.3 0.6 fusion
  6.0 0.9 pad_maximum_fusion
  6.8 110.3 %sync_weights.1 = (f32[3,320,384]{2,1,0:T(8,128)}, bf16[3,8,40,384]{3,2,1,0:T(8,128)(2,1)}, bf16[16,80,896]{2,1,0:T(8,128)(2,1)}, bf16[3072,640]{1,0:T(8,128)(2,1)}) custom-call(f32[3,192,640]{2,1,0:T(8,128)} %bitcast.10, f32[2,864,640]{2,1,0:T(8,128)} %bitcast.9, bf16[320,5120]{1,0:T(8,128)(2,1)} %hid_hbm.1, bf16[384,5120]{1,0:T(8,128)(2,1)} %ow_hbm.1), custom_call_target="tpu_custom_call" | custom-call | flops 3774873600 | bytes 30000000 | tf_op jit(solution)/shard_map/sync_weights/pallas_call | solution.py:439
  117.2 82.3 %attention_layer.1 = (bf16[320,640]{1,0:T(8,128)(2,1)}, bf16[2,5120,384]{2,1,0:T(8,128)(2,1)}, bf16[2,8,40,1728]{3,2,1,0:T(8,128)(2,1)}) custom-call(s32[4]{0:T(128)} %lengths_ref.3, f32[3,320,384]{2,1,0:T(8,128)} %get-tuple-element.11.proj_ref, f32[320,128]{1,0:T(8,128)} %get-tuple-element.25.cos_ref, f32[320,128]{1,0:T(8,128)} %get-tuple-element.26.sin_ref, ...), custom_call_target="tpu_custom_call" | custom-call | flops 8000000000 | bytes 20000000 | tf_op jit(solution)/shard_map/attention_layer/pallas_call | solution.py:686
  199.5 0.0 copy-start.2
  199.5 0.0 copy-start.1
  199.5 7.2 %cache_pages.1 = bf16[16,2,128,384]{3,2,1,0:T(8,128)(2,1)} custom-call(s32[4]{0:T(128)} %lengths_ref.3, s32[4]{0:T(128)} %owner_ref.1, s32[4,16]{1,0:T(4,128)} %table_ref.1, bf16[2,5120,384]{2,1,0:T(8,128)(2,1)} %get-tuple-element.15.kv_hbm), custom_call_target="tpu_custom_call" | custom-call | flops 10000000 | bytes 7000000 | tf_op jit(solution)/shard_map/cache_pages/pallas_call | solution.py:766
  206.7 0.0 copy-start
  206.8 0.0 copy-done.2
  206.8 0.8 copy.16
  207.5 0.0 copy-done.1
  207.5 0.9 copy.17
  208.4 0.3 copy-done
  208.7 1.4 copy.18
  (1 shorter events, 0.0 us)
Async XLA Ops:
  199.5 7.3 %copy-start.2 = (bf16[320,640]{1,0:T(8,128)(2,1)S(1)}, bf16[320,640]{1,0:T(8,128)(2,1)}, u32[]{:S(2)}) copy-start(bf16[320,640]{1,0:T(8,128)(2,1)} %get-tuple-element.31) | copy-start | bytes 1228804
  199.5 8.0 %copy-start.1 = (bf16[3,8,40,384]{3,2,1,0:T(8,128)(2,1)S(1)}, bf16[3,8,40,384]{3,2,1,0:T(8,128)(2,1)}, u32[]{:S(2)}) copy-start(bf16[3,8,40,384]{3,2,1,0:T(8,128)(2,1)} %get-tuple-element.33) | copy-start | bytes 2211844
  206.7 1.9 copy-start

commit v6 on v5

--- a/solution.py
+++ b/solution.py
@@ -547,9 +547,6 @@
     first_sends = Gather(me, True, tokens_of, kv_send, kv_recv)
     first_sends.start(0)
 
-    gate = Relay(me, g2, (g2, g2, g3), g_send, g_recv)
-    gate.third(wait=False)
-
     squares = shared(sq_in, s_send, s_recv)
     cosine, sine = cos_ref[...], sin_ref[...]
     for which in (1, 0):
@@ -564,6 +561,9 @@
                 query[:, lanes] = turned
         if which == 1:
             first_sends.start(1)
+
+    gate = Relay(me, g2, (g2, g2, g3), g_send, g_recv)
+    gate.third(wait=False)
 
     def kv_gather(z_first):
         g = gathers[0 if z_first else 1]

time: 211 us -> 205 us (0.972)
  Pallas kernels: 200 us -> 195 us
    pallas_call x1, Pallas kernels: 82.3 us -> 77.5 us  [attention_layer(): pl.pallas_call(functools.partial(layer_body, n_row=n_row, n_col=n_col), o...]
where the time goes in v6:
time: 205 us
  Pallas kernels  195 us (95%)
  local copies, waits for them, and re-layouts  4.68 us (2%)
  between operations  3.31 us (2%)
  other arithmetic  2.19 us (1%)
    pallas_call x1, Pallas kernels, sync_weights(): pl.pallas_call(functools.partial(sync_body, n_row=n_row, n_col=n_col), ou...  110 us
    pallas_call x1, Pallas kernels, attention_layer(): pl.pallas_call(functools.partial(layer_body, n_row=n_row, n_col=n_col), o...  77.5 us
    pallas_call x1, Pallas kernels, build_cache(): pl.pallas_call(cache_body, out_shape=jax.ShapeDtypeStruct((PAGES, 2, PAGE...  7.24 us

profile of v6, /device:TPU:0, one launch (start us, length us, event | category | flops | bytes accessed | tf_op | source)
XLA Modules:
  0.0 205.2 jit_solution(14984629473917987431)
XLA Ops:
  0.6 1.4 fusion.5
  4.6 0.7 subtract_convert_fusion
  5.3 0.6 fusion
  6.0 0.9 pad_maximum_fusion
  6.8 110.3 %sync_weights.1 = (f32[3,320,384]{2,1,0:T(8,128)}, bf16[3,8,40,384]{3,2,1,0:T(8,128)(2,1)}, bf16[16,80,896]{2,1,0:T(8,128)(2,1)}, bf16[3072,640]{1,0:T(8,128)(2,1)}) custom-call(f32[3,192,640]{2,1,0:T(8,128)} %bitcast.10, f32[2,864,640]{2,1,0:T(8,128)} %bitcast.9, bf16[320,5120]{1,0:T(8,128)(2,1)} %hid_hbm.1, bf16[384,5120]{1,0:T(8,128)(2,1)} %ow_hbm.1), custom_call_target="tpu_custom_call" | custom-call | flops 3774873600 | bytes 30000000 | tf_op jit(solution)/shard_map/sync_weights/pallas_call | solution.py:439
  117.2 77.5 %attention_layer.1 = (bf16[320,640]{1,0:T(8,128)(2,1)}, bf16[2,5120,384]{2,1,0:T(8,128)(2,1)}, bf16[2,8,40,1728]{3,2,1,0:T(8,128)(2,1)}) custom-call(s32[4]{0:T(128)} %lengths_ref.3, f32[3,320,384]{2,1,0:T(8,128)} %get-tuple-element.11.proj_ref, f32[320,128]{1,0:T(8,128)} %get-tuple-element.25.cos_ref, f32[320,128]{1,0:T(8,128)} %get-tuple-element.26.sin_ref, ...), custom_call_target="tpu_custom_call" | custom-call | flops 8000000000 | bytes 20000000 | tf_op jit(solution)/shard_map/attention_layer/pallas_call | solution.py:686
  194.7 0.0 copy-start.2
  194.7 0.0 copy-start.1
  194.7 7.2 %cache_pages.1 = bf16[16,2,128,384]{3,2,1,0:T(8,128)(2,1)} custom-call(s32[4]{0:T(128)} %lengths_ref.3, s32[4]{0:T(128)} %owner_ref.1, s32[4,16]{1,0:T(4,128)} %table_ref.1, bf16[2,5120,384]{2,1,0:T(8,128)(2,1)} %get-tuple-element.15.kv_hbm), custom_call_target="tpu_custom_call" | custom-call | flops 10000000 | bytes 7000000 | tf_op jit(solution)/shard_map/cache_pages/pallas_call | solution.py:766
  201.9 0.0 copy-start
  201.9 0.0 copy-done.2
  202.0 0.8 copy.16
  202.7 0.0 copy-done.1
  202.7 0.9 copy.17
  203.6 0.3 copy-done
  203.8 1.4 copy.18
  (1 shorter events, 0.0 us)
Async XLA Ops:
  194.7 7.3 %copy-start.2 = (bf16[320,640]{1,0:T(8,128)(2,1)S(1)}, bf16[320,640]{1,0:T(8,128)(2,1)}, u32[]{:S(2)}) copy-start(bf16[320,640]{1,0:T(8,128)(2,1)} %get-tuple-element.31) | copy-start | bytes 1228804
  194.7 8.0 %copy-start.1 = (bf16[3,8,40,384]{3,2,1,0:T(8,128)(2,1)S(1)}, bf16[3,8,40,384]{3,2,1,0:T(8,128)(2,1)}, u32[]{:S(2)}) copy-start(bf16[3,8,40,384]{3,2,1,0:T(8,128)(2,1)} %get-tuple-element.33) | copy-start | bytes 2211844
  201.9 1.9 copy-start

commit v7 on v6

--- a/solution.py
+++ b/solution.py
@@ -96,7 +96,7 @@
         me = self.me
 
         def send(i):
-            dx, dk, zh = 3 - i // 4, lax.rem(i // 2, 2), lax.rem(i, 2)
+            dx, dk, zh = i // 4, lax.rem(i // 2, 2), lax.rem(i, 2)
             x, core = lax.rem(me.x + near_first(dx), 4), lax.rem(me.core + dk, 2)
             slot = (me.x * 2 + me.core) * 2 + zh
             away = jnp.logical_or(dx > 0, dk > 0)
@@ -156,7 +156,7 @@
                 ).wait_send()
 
         def each_piece(i):
-            sent(jnp.logical_or(i < 12, lax.rem(i // 2, 2) > 0), 0, i)
+            sent(jnp.logical_or(i >= 4, lax.rem(i // 2, 2) > 0), 0, i)
             xs, zh = i // 4, lax.rem(i, 2)
             sent(jnp.logical_or(lax.rem(xs, 2) != me.zl, zh != me.zh), 1, i)
             zs, xh = i // 4, lax.rem(i // 2, 2)
@@ -591,36 +591,41 @@
     reach = -(-(LMAX - 1) // tok)
     span = min(reach + 1, n_col) * tok
     first_key = pl.multiple_of(jnp.maximum(col - reach, 0) * tok, 64)
-    query_index = col * tok + lax.broadcasted_iota(jnp.int32, (tok, 1), 0)
+    half_tok = tok // 2
     key_index = first_key + lax.broadcasted_iota(jnp.int32, (1, span), 1)
-    prompt_start = jnp.zeros((tok, 1), jnp.int32)
-    end = 0
-    for p in range(lengths_ref.shape[0]):
-        end = end + lengths_ref[p]
-        prompt_start = jnp.where(query_index >= end, end, prompt_start)
-    allowed = (key_index <= query_index) & (key_index >= prompt_start)
-    for head in range(heads):
-        lanes = slice(head * HD, (head + 1) * HD)
+
+    def attend(half):
+        part = slice(half * half_tok, (half + 1) * half_tok)
+        query_index = col * tok + half * half_tok
+        query_index = query_index + lax.broadcasted_iota(jnp.int32, (half_tok, 1), 0)
+        prompt_start = jnp.zeros((half_tok, 1), jnp.int32)
+        end = 0
+        for p in range(lengths_ref.shape[0]):
+            end = end + lengths_ref[p]
+            prompt_start = jnp.where(query_index >= end, end, prompt_start)
+        allowed = (key_index <= query_index) & (key_index >= prompt_start)
+        for head in range(heads):
+            attend_head(part, allowed, slice(head * HD, (head + 1) * HD))
+
+    def attend_head(part, allowed, lanes):
         keys = kv[0, pl.ds(first_key, span), lanes]
         values = kv[1, pl.ds(first_key, span), lanes]
         scores = lax.dot_general(
-            query[:, lanes], keys, (((1,), (1,)), ((), ())), preferred_element_type=f32
+            query[part, lanes], keys, (((1,), (1,)), ((), ())), preferred_element_type=f32
         ) * (1.0 / math.sqrt(HD))
         scores = jnp.where(allowed, scores, big_negative)
         exponent = jnp.exp(scores - jnp.max(scores, axis=1, keepdims=True))
         total = jnp.sum(exponent, axis=1, keepdims=True)
         mixed = jnp.dot(exponent.astype(bf16), values, preferred_element_type=f32)
-        mixed_all[row, :, lanes] = (mixed / total).astype(bf16)
-
-    half_tok = tok // 2
-    row_gathers = [
-        Gather(
-            me, False,
-            lambda block, core, half: mixed_all.at[block, pl.ds(half * half_tok, half_tok), :],
-            a_send, a_recv,
-        )
-        for _ in range(2)
-    ]
+        mixed_all[row, part, lanes] = (mixed / total).astype(bf16)
+
+    def mixed_of(block, core, half):
+        return mixed_all.at[block, pl.ds(half * half_tok, half_tok), :]
+
+    row_gathers = [Gather(me, False, mixed_of, a_send, a_recv) for _ in range(3)]
+    for half in range(2):
+        attend(half)
+        row_gathers[2].start(half)
 
     fine = gblk_ref.shape[2]
 
@@ -630,8 +635,6 @@
 
     def row_gather(z_first):
         g = row_gathers[0 if z_first else 1]
-        g.start(0)
-        g.start(1)
         gate.last()
         each(n_row, gate_join)
         if z_first:
@@ -665,6 +668,7 @@
         row_gathers[which].drain()
 
     by_core(me, drain)
+    row_gathers[2].drain()
     gate.drain((2,))
 
     scale = lax.rsqrt(column_of(shared(sq_out, t_send, t_recv), 0) / (n_row * out_width) + norm_epsilon)

time: 205 us -> 197 us (0.961)
  Pallas kernels: 195 us -> 187 us
    pallas_call x1, Pallas kernels: 77.5 us -> 71.9 us  [attention_layer(): pl.pallas_call(functools.partial(layer_body, n_row=n_row, n_col=n_col), o...]
    pallas_call x1, Pallas kernels: 110 us -> 108 us  [sync_weights(): pl.pallas_call(functools.partial(sync_body, n_row=n_row, n_col=n_col), ou...]
where the time goes in v7:
time: 197 us
  Pallas kernels  187 us (95%)
  local copies, waits for them, and re-layouts  4.68 us (2%)
  between operations  3.31 us (2%)
  other arithmetic  2.19 us (1%)
    pallas_call x1, Pallas kernels, sync_weights(): pl.pallas_call(functools.partial(sync_body, n_row=n_row, n_col=n_col), ou...  108 us
    pallas_call x1, Pallas kernels, attention_layer(): pl.pallas_call(functools.partial(layer_body, n_row=n_row, n_col=n_col), o...  71.9 us
    pallas_call x1, Pallas kernels, build_cache(): pl.pallas_call(cache_body, out_shape=jax.ShapeDtypeStruct((PAGES, 2, PAGE...  7.24 us

profile of v7, /device:TPU:0, one launch (start us, length us, event | category | flops | bytes accessed | tf_op | source)
XLA Modules:
  0.0 197.1 jit_solution(3375938191601150293)
XLA Ops:
  0.6 1.4 fusion.5
  4.6 0.7 subtract_convert_fusion
  5.3 0.6 fusion
  6.0 0.9 pad_maximum_fusion
  6.8 107.8 %sync_weights.1 = (f32[3,320,384]{2,1,0:T(8,128)}, bf16[3,8,40,384]{3,2,1,0:T(8,128)(2,1)}, bf16[16,80,896]{2,1,0:T(8,128)(2,1)}, bf16[3072,640]{1,0:T(8,128)(2,1)}) custom-call(f32[3,192,640]{2,1,0:T(8,128)} %bitcast.10, f32[2,864,640]{2,1,0:T(8,128)} %bitcast.9, bf16[320,5120]{1,0:T(8,128)(2,1)} %hid_hbm.1, bf16[384,5120]{1,0:T(8,128)(2,1)} %ow_hbm.1), custom_call_target="tpu_custom_call" | custom-call | flops 3774873600 | bytes 30000000 | tf_op jit(solution)/shard_map/sync_weights/pallas_call | solution.py:439
  114.7 71.9 %attention_layer.1 = (bf16[320,640]{1,0:T(8,128)(2,1)}, bf16[2,5120,384]{2,1,0:T(8,128)(2,1)}, bf16[2,8,40,1728]{3,2,1,0:T(8,128)(2,1)}) custom-call(s32[4]{0:T(128)} %lengths_ref.3, f32[3,320,384]{2,1,0:T(8,128)} %get-tuple-element.11.proj_ref, f32[320,128]{1,0:T(8,128)} %get-tuple-element.25.cos_ref, f32[320,128]{1,0:T(8,128)} %get-tuple-element.26.sin_ref, ...), custom_call_target="tpu_custom_call" | custom-call | flops 8000000000 | bytes 20000000 | tf_op jit(solution)/shard_map/attention_layer/pallas_call | solution.py:690
  186.6 0.0 copy-start.2
  186.6 0.0 copy-start.1
  186.6 7.2 %cache_pages.1 = bf16[16,2,128,384]{3,2,1,0:T(8,128)(2,1)} custom-call(s32[4]{0:T(128)} %lengths_ref.3, s32[4]{0:T(128)} %owner_ref.1, s32[4,16]{1,0:T(4,128)} %table_ref.1, bf16[2,5120,384]{2,1,0:T(8,128)(2,1)} %get-tuple-element.15.kv_hbm), custom_call_target="tpu_custom_call" | custom-call | flops 10000000 | bytes 7000000 | tf_op jit(solution)/shard_map/cache_pages/pallas_call | solution.py:770
  193.8 0.0 copy-start
  193.9 0.0 copy-done.2
  193.9 0.8 copy.16
  194.6 0.0 copy-done.1
  194.6 0.9 copy.17
  195.5 0.3 copy-done
  195.8 1.4 copy.18
  (1 shorter events, 0.0 us)
Async XLA Ops:
  186.6 7.3 %copy-start.2 = (bf16[320,640]{1,0:T(8,128)(2,1)S(1)}, bf16[320,640]{1,0:T(8,128)(2,1)}, u32[]{:S(2)}) copy-start(bf16[320,640]{1,0:T(8,128)(2,1)} %get-tuple-element.31) | copy-start | bytes 1228804
  186.6 8.0 %copy-start.1 = (bf16[3,8,40,384]{3,2,1,0:T(8,128)(2,1)S(1)}, bf16[3,8,40,384]{3,2,1,0:T(8,128)(2,1)}, u32[]{:S(2)}) copy-start(bf16[3,8,40,384]{3,2,1,0:T(8,128)(2,1)} %get-tuple-element.33) | copy-start | bytes 2211844
  193.8 1.9 copy-start

commit v8 on v7

--- a/solution.py
+++ b/solution.py
@@ -635,17 +635,19 @@
 
     def row_gather(z_first):
         g = row_gathers[0 if z_first else 1]
-        gate.last()
-        each(n_row, gate_join)
         if z_first:
             g.z_turn()
             g.x_turn(0)
             g.x_turn(1)
+            gate.last()
+            each(n_row, gate_join)
             g.x_end(0)
             g.x_end(1)
         else:
             g.x_turn(0, 2)
             g.x_end(0, 2)
+            gate.last()
+            each(n_row, gate_join)
             g.z_end()
 
     by_core(me, row_gather)

time: 197 us -> 197 us (level)
  no operation moved by 1% of the time
where the time goes in v8:
time: 197 us
  Pallas kernels  187 us (95%)
  local copies, waits for them, and re-layouts  4.68 us (2%)
  between operations  3.31 us (2%)
  other arithmetic  2.19 us (1%)
    pallas_call x1, Pallas kernels, sync_weights(): pl.pallas_call(functools.partial(sync_body, n_row=n_row, n_col=n_col), ou...  108 us
    pallas_call x1, Pallas kernels, attention_layer(): pl.pallas_call(functools.partial(layer_body, n_row=n_row, n_col=n_col), o...  71.9 us
    pallas_call x1, Pallas kernels, build_cache(): pl.pallas_call(cache_body, out_shape=jax.ShapeDtypeStruct((PAGES, 2, PAGE...  7.24 us

profile of v8, /device:TPU:0, one launch (start us, length us, event | category | flops | bytes accessed | tf_op | source)
XLA Modules:
  0.0 197.1 jit_solution(16391677609572886086)
XLA Ops:
  0.6 1.4 fusion.5
  4.6 0.7 subtract_convert_fusion
  5.3 0.6 fusion
  6.0 0.9 pad_maximum_fusion
  6.8 107.8 %sync_weights.1 = (f32[3,320,384]{2,1,0:T(8,128)}, bf16[3,8,40,384]{3,2,1,0:T(8,128)(2,1)}, bf16[16,80,896]{2,1,0:T(8,128)(2,1)}, bf16[3072,640]{1,0:T(8,128)(2,1)}) custom-call(f32[3,192,640]{2,1,0:T(8,128)} %bitcast.10, f32[2,864,640]{2,1,0:T(8,128)} %bitcast.9, bf16[320,5120]{1,0:T(8,128)(2,1)} %hid_hbm.1, bf16[384,5120]{1,0:T(8,128)(2,1)} %ow_hbm.1), custom_call_target="tpu_custom_call" | custom-call | flops 3774873600 | bytes 30000000 | tf_op jit(solution)/shard_map/sync_weights/pallas_call | solution.py:439
  114.7 71.9 %attention_layer.1 = (bf16[320,640]{1,0:T(8,128)(2,1)}, bf16[2,5120,384]{2,1,0:T(8,128)(2,1)}, bf16[2,8,40,1728]{3,2,1,0:T(8,128)(2,1)}) custom-call(s32[4]{0:T(128)} %lengths_ref.3, f32[3,320,384]{2,1,0:T(8,128)} %get-tuple-element.11.proj_ref, f32[320,128]{1,0:T(8,128)} %get-tuple-element.25.cos_ref, f32[320,128]{1,0:T(8,128)} %get-tuple-element.26.sin_ref, ...), custom_call_target="tpu_custom_call" | custom-call | flops 8000000000 | bytes 20000000 | tf_op jit(solution)/shard_map/attention_layer/pallas_call | solution.py:692
  186.6 0.0 copy-start.2
  186.6 0.0 copy-start.1
  186.6 7.2 %cache_pages.1 = bf16[16,2,128,384]{3,2,1,0:T(8,128)(2,1)} custom-call(s32[4]{0:T(128)} %lengths_ref.3, s32[4]{0:T(128)} %owner_ref.1, s32[4,16]{1,0:T(4,128)} %table_ref.1, bf16[2,5120,384]{2,1,0:T(8,128)(2,1)} %get-tuple-element.15.kv_hbm), custom_call_target="tpu_custom_call" | custom-call | flops 10000000 | bytes 7000000 | tf_op jit(solution)/shard_map/cache_pages/pallas_call | solution.py:772
  193.8 0.0 copy-start
  193.9 0.0 copy-done.2
  193.9 0.8 copy.16
  194.6 0.0 copy-done.1
  194.6 0.9 copy.17
  195.5 0.3 copy-done
  195.8 1.4 copy.18
  (1 shorter events, 0.0 us)
Async XLA Ops:
  186.6 7.3 %copy-start.2 = (bf16[320,640]{1,0:T(8,128)(2,1)S(1)}, bf16[320,640]{1,0:T(8,128)(2,1)}, u32[]{:S(2)}) copy-start(bf16[320,640]{1,0:T(8,128)(2,1)} %get-tuple-element.31) | copy-start | bytes 1228804
  186.6 8.0 %copy-start.1 = (bf16[3,8,40,384]{3,2,1,0:T(8,128)(2,1)S(1)}, bf16[3,8,40,384]{3,2,1,0:T(8,128)(2,1)}, u32[]{:S(2)}) copy-start(bf16[3,8,40,384]{3,2,1,0:T(8,128)(2,1)} %get-tuple-element.33) | copy-start | bytes 2211844
  193.8 1.9 copy-start
